TPU v7x, 32 devices: a whole 2x2x4 slice. The times are simulated.
32 devices in a mesh: seq: 8 (over y, x, core), tp: 4 (over z).
Axes of the slice: x: 2, y: 2, z: 4, core: 2. Of those that a mesh axis runs over, the one named last changes fastest.
Arguments:
- tokens: bfloat16 [128, 17, 1152], P('seq'), may hold values from -6 to 6
- cotangent: bfloat16 [128, 17, 1152], P('seq'), may hold values from -6 to 6
- caption: bfloat16 [4, 300, 1152], replicated, may hold values from -6 to 6
- condition: float32 [4, 1152], replicated, may hold values from -6 to 6
- frames: int32 [4], replicated, may hold values from 1 to 17, 44 in all
- cap_len: int32 [4], replicated, may hold values from 1 to 300, 600 in all
- clip_of: int32 [128], P('seq'), may hold values from 0 to 3
- w_qkv: bfloat16 [1152, 3, 1152], P('seq', None, 'tp'), may hold values from -0.1875 to 0.1875
- w_out: bfloat16 [1152, 1152], P('tp', 'seq'), may hold values from -0.375 to 0.375
- w_query2: bfloat16 [1152, 1152], P('seq', 'tp'), may hold values from -0.1875 to 0.1875
- w_kv2: bfloat16 [1152, 2, 1152], P('seq', None, 'tp'), may hold values from -0.1875 to 0.1875
- w_out2: bfloat16 [1152, 1152], P('tp', 'seq'), may hold values from -0.75 to 0.75
- w_up: bfloat16 [1152, 4608], P('seq', 'tp'), may hold values from -0.1875 to 0.1875
- w_down: bfloat16 [4608, 1152], P('tp', 'seq'), may hold values from -0.09375 to 0.09375
- w_ada: bfloat16 [1152, 6912], P('seq', 'tp'), may hold values from -0.1875 to 0.1875
Outputs:
- output: bfloat16 [128, 17, 1152], P('seq')
- d_tokens: bfloat16 [128, 17, 1152], P('seq')
- d_caption: float32 [4, 300, 1152], P(None, None, 'tp')
- d_condition: float32 [4, 1152], replicated
- d_w_qkv: float32 [1152, 3, 1152], P('seq', None, 'tp')
- d_w_out: float32 [1152, 1152], P('tp', 'seq')
- d_w_query2: float32 [1152, 1152], P('seq', 'tp')
- d_w_kv2: float32 [1152, 2, 1152], P('seq', None, 'tp')
- d_w_out2: float32 [1152, 1152], P('tp', 'seq')
- d_w_up: float32 [1152, 4608], P('seq', 'tp')
- d_w_down: float32 [4608, 1152], P('tp', 'seq')
- d_w_ada: float32 [1152, 6912], P('seq', 'tp')
Inputs may be any that keep to these rules, and one draw needn't show every extreme that they name: frames of each clip; they add up to 44 and one clip has 17. `cap_len`: live caption tokens of each clip, the first ones of its slots; they add up to 600 and one clip has 300.
All inputs are finite; a program needn't handle non-finite values.
Results may differ from a plain program's by a relative error of at most 0.024.
Values may be sent and summed in bfloat16 or wider, within the bound.
No kernel may reach another device: no remote copies, remote signals or barrier semaphores. Data moves between devices by JAX's collectives and lax.ppermute only.
A program may use at most 128 MiB of HBM per device.

v0:
```python
import functools
import math

import jax
import jax.numpy as jnp
from jax import lax
from jax.experimental import pallas as pl
from jax.experimental.pallas import tpu as pltpu
from jax.sharding import PartitionSpec as P

HDIM = 72
EPSILON = 1e-06
NEG_FILL = -1e30
F32 = jnp.float32
BF16 = jnp.bfloat16
SCALE = HDIM ** (-0.5)
VMEM_LIMIT = 48 << 20


def dot_nn(a, b):
    return lax.dot_general(a, b, (((1,), (0,)), ((), ())), preferred_element_type=F32)


def dot_nt(a, b):
    return lax.dot_general(a, b, (((1,), (1,)), ((), ())), preferred_element_type=F32)


def dot_tn(a, b):
    return lax.dot_general(a, b, (((0,), (0,)), ((), ())), preferred_element_type=F32)


def sds(shape, dtype=BF16):
    return jax.ShapeDtypeStruct(shape, dtype)


class Blocks:
    def __init__(self, pieces):
        self.pieces = pieces


class Cols:
    def __init__(self, whole, start, size):
        self.whole, self.start, self.size = whole, start, size


class Near:
    def __init__(self, whole):
        self.whole = whole


class Half:
    def __init__(self, shape, start, size):
        self.shape, self.dtype, self.start, self.size = shape, BF16, start, size


class In:
    def __init__(self, buf, copies):
        self.buf, self.copies, self.ready = buf, copies, not copies

    @property
    def shape(self):
        return self.buf.shape

    def ref(self):
        if not self.ready:
            for copy in self.copies:
                copy.wait()
            self.ready = True
        return self.buf

    def __getitem__(self, index):
        return self.ref()[index]


class Out:
    def __init__(self, bufs, copies):
        self.bufs, self.copies, self.sent = bufs, copies, False

    @property
    def shape(self):
        return self.bufs[0].shape

    def __getitem__(self, index):
        return self.bufs[0][index]

    def __setitem__(self, index, value):
        self.bufs[0][index] = value

    def send(self):
        if not self.sent:
            for copy in self.copies:
                copy.start()
            self.sent = True


def call(body, outs, ins, *, name, smem=(), order=(), keep=False, work=(), limit=VMEM_LIMIT):
    vmem, hbm = pl.BlockSpec(memory_space=pltpu.VMEM), pl.BlockSpec(memory_space=pltpu.HBM)
    pin = lambda value: pltpu.with_memory_space_constraint(value, pltpu.HBM)
    ops, in_specs, in_plan, scratch_in = [], [], [], []
    n_in = 0
    for arg in ins:
        if isinstance(arg, Near):
            in_plan.append((len(ops), None, arg, 0))
            ops.append(arg.whole)
            in_specs.append(vmem)
            continue
        pieces = arg.pieces if isinstance(arg, Blocks) else [arg.whole if isinstance(arg, Cols) else arg]
        shape = pieces[0].shape
        if isinstance(arg, Blocks):
            shape = (shape[0] * len(pieces),) + shape[1:]
        elif isinstance(arg, Cols):
            shape = (shape[0], arg.size)
        in_plan.append((len(ops), len(scratch_in), arg, n_in))
        scratch_in.append(pltpu.VMEM(shape, pieces[0].dtype))
        n_in += len(pieces)
        ops += [pin(p) for p in pieces]
        in_specs += [hbm] * len(pieces)
    n_read = len(ops)
    for arg in order:
        ops.append(arg.whole if isinstance(arg, Near) else pin(arg))
        in_specs.append(vmem if isinstance(arg, Near) else hbm)
    results, out_plan, scratch_out = [], [], []
    n_out = 0
    for out in outs:
        out_plan.append((len(results), len(scratch_out), out, n_out))
        results.append(out)
        wide = (out.shape[0], out.size) if isinstance(out, Half) else out.shape
        scratch_out.append(pltpu.VMEM(wide, out.dtype))
        n_out += 1
    n_s, n_i, n_o = len(smem), len(ops), len(results)

    def kernel(*refs):
        scalars = refs[:n_s]
        src = refs[n_s : n_s + n_read]
        dst = refs[n_s + n_i : n_s + n_i + n_o]
        scratch = refs[n_s + n_i + n_o :]
        bufs = scratch[: len(scratch_in)]
        obufs = scratch[len(scratch_in) : len(scratch_in) + len(scratch_out)]
        extra = list(scratch[len(scratch_in) + len(scratch_out) : -2])
        in_sem, out_sem = scratch[-2:]
        lazy = []
        for start, at, arg, sem in in_plan:
            if at is None:
                lazy.append(In(src[start], []))
                continue
            copies = []
            if isinstance(arg, Blocks):
                rows = src[start].shape[0]
                for m in range(len(arg.pieces)):
                    block = lax.bitwise_xor(scalars[0][1], m)
                    place = bufs[at].at[pl.ds(pl.multiple_of(block * rows, 8), rows)]
                    copies.append(pltpu.make_async_copy(src[start + m], place, in_sem.at[sem + m]))
            else:
                part = src[start]
                if isinstance(arg, Cols):
                    part = part.at[:, pl.ds(arg.start, arg.size)]
                copies.append(pltpu.make_async_copy(part, bufs[at], in_sem.at[sem]))
            for copy in copies:
                copy.start()
            lazy.append(In(bufs[at], copies))
        made = []
        for first, at, out, sem in out_plan:
            place = dst[first]
            if isinstance(out, Half):
                place = place.at[:, pl.ds(out.start, out.size)]
            copy = pltpu.make_async_copy(obufs[at], place, out_sem.at[sem])
            made.append(Out([obufs[at]], [copy]))
        body(scalars, lazy, made + extra)
        for item in lazy:
            if not item.ready:
                item[...]
        for out in made:
            out.send()
        for out in made:
            for copy in out.copies:
                copy.wait()

    moved = sum(a.size * a.dtype.itemsize for a in ops[:n_read])
    moved += sum(math.prod(o.shape) * jnp.dtype(o.dtype).itemsize for o in results)
    return pl.pallas_call(
        kernel,
        out_shape=tuple(pltpu.HBM(o.shape, o.dtype) for o in results),
        in_specs=[pl.BlockSpec(memory_space=pltpu.SMEM)] * n_s + in_specs,
        out_specs=tuple([hbm] * n_o),
        scratch_shapes=scratch_in
        + scratch_out
        + [pltpu.VMEM(w.shape, w.dtype) for w in work]
        + [pltpu.SemaphoreType.DMA((max(n_in, 1),)), pltpu.SemaphoreType.DMA((max(n_out, 1),))],
        input_output_aliases={n_s + n_read: 0} if keep else {},
        compiler_params=pltpu.CompilerParams(vmem_limit_bytes=limit),
        cost_estimate=pl.CostEstimate(flops=0, transcendentals=0, bytes_accessed=moved),
        name=name,
    )(*smem, *ops)


def norm_parts(rows):
    center = rows - jnp.mean(rows, -1, keepdims=True)
    inv = lax.rsqrt(jnp.mean(center * center, -1, keepdims=True) + EPSILON)
    return center * inv, inv


def expand(hot, table):
    high = table.astype(BF16)
    low = (table - high.astype(F32)).astype(BF16)
    return dot_nn(hot, high) + dot_nn(hot, low)


def split_dot(dot, a, b):
    high = a.astype(BF16)
    low = (a - high.astype(F32)).astype(BF16)
    return dot(high, b) + dot(low, b)


def clip_sums(clips_hot, values):
    return dot_nn(clips_hot, values.astype(BF16))


def norm_back(grad, n, inv):
    return inv * (grad - jnp.mean(grad, -1, keepdims=True) - n * jnp.mean(grad * n, -1, keepdims=True))


def softmax_rows(scores):
    top = jnp.max(scores, -1, keepdims=True)
    weights = jnp.exp(scores - top)
    return weights / jnp.sum(weights, -1, keepdims=True)


def pack_rows(out, value, tp):
    own, n = value.shape[0] // tp, value.shape[1]
    for r in range(tp):
        out[:, r * n : (r + 1) * n] = value[r * own : (r + 1) * own]


def unpack_heads(pieces, tp, n):
    pieces = [p[...] for p in pieces]
    rows = []
    for b in range(tp):
        cols = []
        for k in range(tp):
            r = (b - k) % tp
            cols.append(pieces[k][:, r * n : (r + 1) * n])
        rows.append(jnp.concatenate(cols, axis=1))
    return jnp.concatenate(rows, axis=0)


def far(parts):
    return [parts[0]] + [Near(p) for p in parts[1:]]


def put_heads(work, value, start=0):
    for h in range(work.shape[0]):
        work[h] = value[:, start + h * HDIM : start + (h + 1) * HDIM]


def take_heads(work):
    return jnp.concatenate([work[h] for h in range(work.shape[0])], axis=1)


def for_heads(count, body):
    def step(h, carry):
        body(h)
        return carry

    lax.fori_loop(0, count, step, 0)


def for_columns(width, body, most=384):
    size = math.gcd(width, most)

    def step(i, carry):
        body(pl.ds(pl.multiple_of(i * size, size), size))
        return carry

    lax.fori_loop(0, width // size, step, 0)


def total(parts):
    value = parts[0][...].astype(F32)
    for part in parts[1:]:
        value = value + part[...].astype(F32)
    return value


def prepare_rows(tp, scalars, ins, outs):
    rank, clip_of, frames = scalars
    tok_o, g3_o, hot_o, clip_o, id_o, key_o, live_o, turned_o, canon = outs
    rows, width = tok_o.shape
    own = rows // tp
    fmax, seqs = ins[0].shape[:2]
    own_seqs = seqs // tp
    used = own_seqs * fmax
    row = lax.broadcasted_iota(jnp.int32, (own, 1), 0)
    spot = lax.rem(row, own_seqs)
    place = lax.broadcasted_iota(jnp.int32, key_o.shape, 1)
    keys = jnp.full(key_o.shape, -2, jnp.int32)
    owner = jnp.full(key_o.shape, -1, jnp.int32)
    alive = []
    for k in range(tp):
        base = lax.rem(rank[0] - k + tp, tp) * own_seqs
        at = slice(k * own, (k + 1) * own)
        clip = jnp.full((own, 1), -1, jnp.int32)
        name = jnp.full((own, 1), -1, jnp.int32)
        limit = jnp.zeros((own, 1), jnp.int32)
        inside = place - k * own
        mine = (inside >= 0) & (inside < used)
        turn = lax.rem(jnp.maximum(inside, 0), own_seqs)
        for j in range(own_seqs):
            c = clip_of[base + j]
            count = frames[c] * own_seqs
            here = (spot == j) & (row < used)
            clip = jnp.where(here, c, clip)
            name = jnp.where(here, k * own_seqs + j, name)
            limit = jnp.where(here, count, limit)
            there = mine & (turn == j)
            owner = jnp.where(there, c, owner)
            keys = jnp.where(there & (inside < count), k * own_seqs + j, keys)
        live = jnp.where(row < limit, 1.0, 0.0)
        alive.append(live)
        live_o[at] = live
        clip_o[at] = clip
        id_o[at] = name
        lane = lax.broadcasted_iota(jnp.int32, (own, hot_o.shape[1]), 1)
        hot_o[at] = jnp.where(lane == clip, 1.0, 0.0).astype(BF16)
    key_o[...] = keys
    which = lax.broadcasted_iota(jnp.int32, turned_o.shape, 0)
    turned_o[...] = jnp.where(which == owner, 1.0, 0.0).astype(BF16)
    for source, out, mask in ((ins[0], tok_o, False), (ins[1], g3_o, True)):
        if own > used:
            canon[:, used:] = jnp.zeros((tp, own - used, width), BF16)
        for f in range(fmax):
            for q in range(tp):
                group = source[f, q * own_seqs : (q + 1) * own_seqs]
                canon[q, f * own_seqs : (f + 1) * own_seqs] = group
        for k in range(tp):
            value = canon[lax.rem(rank[0] - k + tp, tp)]
            if mask:
                value = (value.astype(F32) * alive[k]).astype(BF16)
            out[k * own : (k + 1) * own] = value
        out.send()


def live_captions(scalars, ins, outs):
    (cap_len,) = scalars
    (caption,) = ins
    cap_o, clip_o = outs
    keys = cap_o.shape[0]
    clips, slots = caption.shape[:2]
    col = lax.broadcasted_iota(jnp.int32, (1, keys), 1)
    clip = jnp.full((1, keys), -9, jnp.int32)
    start = jnp.int32(0)
    spans = []
    for c in range(clips):
        end = start + cap_len[c]
        clip = jnp.where((col >= start) & (col < end), c, clip)
        spans.append((start, end))
        start = end
    clip_o[...] = clip
    source, target = caption.ref(), cap_o.bufs[0]
    step = math.gcd(keys, 128)

    def some(i, carry):
        row = lax.broadcasted_iota(jnp.int32, (step, slots), 0) + i * step
        slot = lax.broadcasted_iota(jnp.int32, (step, slots), 1)
        value = jnp.zeros((step, target.shape[1]), F32)
        for c, (begin, end) in enumerate(spans):
            pick = (row - begin == slot) & (row < end)
            value = value + dot_nn(jnp.where(pick, 1.0, 0.0).astype(BF16), source[c])
        target[pl.ds(pl.multiple_of(i * step, step), step)] = value.astype(BF16)
        return carry

    lax.fori_loop(0, keys // step, some, 0)


def modulations(tp, clips, first, scalars, ins, outs):
    (rank,) = scalars
    (mods_o,) = outs
    width = mods_o.shape[2]
    groups = (ins[0].shape[0] - first) // (2 * clips)

    def joined(ref):
        cols = []
        for g in range(groups):
            at = first + g * clips
            high = ref[at : at + clips].astype(F32)
            cols.append(high + ref[at + groups * clips : at + (groups + 1) * clips].astype(F32))
        return jnp.concatenate(cols, axis=1)

    parts = [joined(ref) for ref in ins]
    cols = []
    for q in range(tp):
        value = parts[0]
        for k in range(1, tp):
            value = jnp.where(lax.rem(rank[0] - k + tp, tp) == q, parts[k], value)
        cols.append(value)
    whole = jnp.concatenate(cols, axis=1)
    mods_o[...] = jnp.zeros(mods_o.shape, F32)
    for j in range(6):
        mods_o[j, :clips] = whole[:, j * width : (j + 1) * width]


def frame_forward(tp, scalars, ins, outs):
    tok, hot, mods, row_id, key_id, w_a = ins
    attn_o, qkv_o, prob_o, fo_o = outs[:4]
    branch_o = outs[4:-2]
    heads, made = outs[-2:]
    inner = fo_o.shape[1]
    own = branch_o[0].shape[0]
    n, _ = norm_parts(tok[...].astype(F32))
    low = (n * (1.0 + expand(hot[...], mods[1])) + expand(hot[...], mods[0])).astype(BF16)
    attn_o[...] = low
    attn_o.send()
    qkv = dot_nn(low, w_a[:, : 3 * inner]).astype(BF16)
    qkv_o[...] = qkv
    qkv_o.send()
    allowed = row_id[...] == key_id[...]
    for i in range(3):
        put_heads(heads.at[i], qkv, i * inner)
    prob = prob_o.bufs[0]

    def one(h):
        scores = dot_nt(heads[0, h], heads[1, h]) * SCALE
        probs = softmax_rows(jnp.where(allowed, scores, NEG_FILL)).astype(BF16)
        prob[h] = probs
        made[h] = dot_nn(probs, heads[2, h]).astype(BF16)

    for_heads(inner // HDIM, one)
    result = take_heads(made)
    prob_o.send()
    fo_o[...] = result
    fo_o.send()
    weights, low_out = w_a.ref(), fo_o.bufs[0]

    def last(cols):
        branch = dot_nt(low_out[...], weights[cols, 3 * inner : 4 * inner]).astype(BF16)
        for r in range(tp):
            branch_o[r].bufs[0][:, cols] = branch[r * own : (r + 1) * own]

    for_columns(weights.shape[0], last)
    for out in branch_o:
        out.send()


def first_rows(tp, scalars, ins, outs):
    tok, hot, mods = ins[tp:]
    x1_o, low_o, branch_o = outs
    own = x1_o.shape[0]
    gate = expand(hot[:own], mods[2])
    branch = total(ins[:tp])
    branch_o[...] = branch
    branch_o.send()
    first = tok[:own].astype(F32) + gate * branch
    x1_o[...] = first
    low_o[...] = first.astype(BF16)


def key_values(scalars, ins, outs):
    cap, w_kv = (item.ref() for item in ins)
    kv = outs[0].bufs[0]
    step = math.gcd(kv.shape[0], 128)

    def some(i, carry):
        at = pl.ds(pl.multiple_of(i * step, 16), step)
        kv[at] = dot_nn(cap[at], w_kv[...]).astype(BF16)
        return carry

    lax.fori_loop(0, kv.shape[0] // step, some, 0)


def cross_forward(tp, inner, scalars, ins, outs):
    row_clip, key_clip, w_q2, kv = ins[tp:]
    low_o, cq_o, prob_o, co_o, pack_o, query, pair, made = outs
    low = jnp.concatenate([r[...] for r in ins[:tp]], axis=0)
    low_o[...] = low
    low_o.send()
    cq = dot_nn(low, w_q2[:, :inner]).astype(BF16)
    cq_o[...] = cq
    cq_o.send()
    allowed = row_clip[...] == key_clip[...]
    put_heads(query, cq)
    for i in range(2):
        put_heads(pair.at[i], kv.ref(), i * inner)
    prob = prob_o.bufs[0]

    def one(h):
        scores = jnp.where(allowed, dot_nt(query[h], pair[0, h]) * SCALE, NEG_FILL)
        probs = softmax_rows(scores).astype(BF16)
        prob[h] = probs
        made[h] = dot_nn(probs, pair[1, h]).astype(BF16)

    for_heads(inner // HDIM, one)
    result = take_heads(made)
    pack_rows(pack_o, result, tp)
    pack_o.send()
    prob_o.send()
    co_o[...] = result


GELU_C = 0.7978845608028654


def mlp_both(tp, inner, scalars, ins, outs):
    pieces = ins[:tp]
    first, low_first, g3, hot, mods, w_out2, w_up, w_down, turned = ins[tp:]
    x2_o, mlp_o, hid_o, db3_o, dpre_o, sums_o = outs[:6]
    dm_o, b3_o = outs[6 : 6 + tp], outs[6 + tp :]
    own, width = x2_o.shape
    hid = hid_o.shape[1]
    d_b3 = (expand(hot[...], mods[5]) * g3[...].astype(F32)).astype(BF16)
    db3_o[...] = d_b3
    db3_o.send()
    rows = unpack_heads(pieces, tp, inner)
    branch = dot_nt(rows, w_out2[...])
    second = jnp.concatenate(
        [first[...] + branch[:own], low_first[own:].astype(F32) + branch[own:]], axis=0
    )
    x2_o[...] = second[:own]
    x2_o.send()
    n, _ = norm_parts(second)
    mlp_o[...] = (n * (1.0 + expand(hot[...], mods[4])) + expand(hot[...], mods[3])).astype(BF16)
    mlp_o.send()
    low, d_low, hiddens, d_pres = (o.bufs[0] for o in (mlp_o, db3_o, hid_o, dpre_o))
    up, down = w_up.ref(), w_down.ref()

    def some(cols):
        pre = dot_nn(low[...], up[:, cols])
        th = jnp.tanh(GELU_C * (pre + 0.044715 * (pre * pre * pre)))
        hiddens[:, cols] = (0.5 * pre * (1.0 + th)).astype(BF16)
        slope = 0.5 * (1.0 + th) + 0.5 * pre * (1.0 - th * th) * (
            GELU_C * (1.0 + 3.0 * 0.044715 * (pre * pre))
        )
        d_pres[:, cols] = (slope * dot_nn(d_low[...], down[:, cols])).astype(BF16)

    if hid % 128:
        some(slice(0, hid))
    else:
        for_columns(hid, some)
    hid_o.send()
    dpre_o.send()
    turn, held, found = turned[...], g3.ref(), sums_o.bufs[0]

    def back(cols):
        d_m = dot_nt(d_pres[...], up[cols, :hid]).astype(BF16)
        for r in range(tp):
            dm_o[r].bufs[0][:, cols] = d_m[r * own : (r + 1) * own]

    for_columns(width, back)
    for out in dm_o:
        out.send()

    def ahead(cols):
        b3 = dot_nt(hiddens[...], down[cols, :hid]).astype(BF16)
        for r in range(tp):
            b3_o[r].bufs[0][:, cols] = b3[r * own : (r + 1) * own]
        found[:, cols] = clip_sums(turn, b3.astype(F32) * held[:, cols].astype(F32))

    for_columns(width, ahead)


def second_back(tp, scalars, ins, outs):
    x2, g3, hot, mods, turned = ins[tp:]
    g2_o, db2_o, sums_o = outs
    own = g2_o.shape[0]
    n, inv = norm_parts(x2[...])
    scale = 1.0 + expand(hot[:own], mods[4])
    d_m = total(ins[:tp])
    g2 = g3[:own].astype(F32) + norm_back(d_m * scale, n, inv)
    db2_o[...] = g2.astype(BF16)
    db2_o.send()
    g2_o[...] = g2
    sums_o[0] = clip_sums(turned[:, :own], d_m)
    sums_o[1] = clip_sums(turned[:, :own], d_m * n)


def cross_back(tp, inner, scalars, ins, outs):
    (rank,) = scalars
    w_out2, prob, kv, cq = ins[tp:]
    db2_o, dcq_o, dkv_o, pack_o, rel_o, query, pair, grads, made, scores, back = outs
    d_b2 = jnp.concatenate([r[...] for r in ins[:tp]], axis=0)
    db2_o[...] = d_b2
    db2_o.send()
    d_co = dot_nn(d_b2, w_out2[:, :inner]).astype(BF16)
    put_heads(grads, d_co)
    put_heads(query, cq.ref())
    for i in range(2):
        put_heads(pair.at[i], kv.ref(), i * inner)
    probs = prob.ref()

    def one(h):
        wide = probs[h].astype(F32)
        d_p = dot_nt(grads[h], pair[1, h])
        d_s = (wide * (d_p - jnp.sum(wide * d_p, -1, keepdims=True))).astype(BF16)
        scores[h] = d_s
        made[h] = (dot_nn(d_s, pair[0, h]) * SCALE).astype(BF16)

    for_heads(inner // HDIM, one)
    result = take_heads(made)
    pack_rows(pack_o, result, tp)
    pack_o.send()
    dcq_o[...] = result
    dcq_o.send()

    def two(h):
        back[0, h] = (dot_tn(scores[h], query[h]) * SCALE).astype(BF16)
        back[1, h] = dot_tn(probs[h], grads[h]).astype(BF16)

    for_heads(inner // HDIM, two)
    d_kv = jnp.concatenate([take_heads(back.at[0]), take_heads(back.at[1])], axis=1)
    blocks, size = rel_o.shape[:2]
    for b in range(blocks):
        other = lax.bitwise_xor(rank[1], b)
        rel_o[(other % 2) * (blocks // 2) + other // 2] = d_kv[b * size : (b + 1) * size]
    rel_o.send()
    dkv_o[...] = d_kv


def frame_back(tp, inner, scalars, ins, outs):
    pieces = ins[:tp]
    (rank,) = scalars
    d_b2, g2, hot, mods, w_q2, w_far, w_a, qkv, prob, tok, own_b1, sums, gate2, turned = ins[tp:]
    g1_o, db1_o, dqkv_o = outs[:3]
    da_o = outs[3:-6]
    heads, grads, made, cqs, norms, found = outs[-6:]
    own, width = g1_o.shape
    d_cq = unpack_heads(pieces, tp, inner)
    cqs[...] = d_cq
    near_w, far_w, held, second, table = (r.ref() for r in (w_q2, w_far, d_b2, g2, mods))
    pick = hot[...]
    g1s, d_b1s = g1_o.bufs[0], db1_o.bufs[0]

    def first(cols):
        d_x1 = dot_nt(cqs[:, :inner], near_w[cols, :inner]) + dot_nt(cqs[:, inner:], far_w[cols])
        g1s[:, cols] = second[:, cols] + d_x1[:own]
        gate = expand(pick, table[2, :, cols])
        d_b1s[:, cols] = (gate * (held[:, cols].astype(F32) + d_x1)).astype(BF16)

    for_columns(width, first)
    g1_o.send()
    db1_o.send()
    d_fo = dot_nn(d_b1s[...], w_a[:, 3 * inner : 4 * inner]).astype(BF16)
    put_heads(grads, d_fo)
    for i in range(3):
        put_heads(heads.at[i], qkv.ref(), i * inner)
    probs = prob.ref()

    def one(h):
        grad = grads[h]
        wide = probs[h].astype(F32)
        made[2, h] = dot_tn(probs[h], grad).astype(BF16)
        d_p = dot_nt(grad, heads[2, h])
        d_s = (wide * (d_p - jnp.sum(wide * d_p, -1, keepdims=True))).astype(BF16)
        made[0, h] = (dot_nn(d_s, heads[1, h]) * SCALE).astype(BF16)
        made[1, h] = (dot_tn(d_s, heads[0, h]) * SCALE).astype(BF16)

    for_heads(inner // HDIM, one)
    d_qkv = jnp.concatenate([take_heads(made.at[i]) for i in range(3)], axis=1)
    dqkv_o[...] = d_qkv
    d_qkvs = dqkv_o.bufs[0]
    dqkv_o.send()
    n, _ = norm_parts(tok[...].astype(F32))
    norms[...] = n
    weights, turn, extra = w_a.ref(), turned[...], own_b1.ref()

    def last(cols):
        low = dot_nt(d_qkvs[...], weights[cols, : 3 * inner]).astype(BF16)
        for r in range(tp):
            da_o[r].bufs[0][:own, cols] = low[r * own : (r + 1) * own]
        found[0, :, cols] = dot_nn(turn, low)
        found[1, :, cols] = clip_sums(turn, low.astype(F32) * norms[:, cols])
        found[2, :, cols] = clip_sums(turn[:, :own], g1s[:, cols] * extra[:, cols])

    for_columns(width, last)
    shift, scale, gate1 = found[0], found[1], found[2]
    whole = jnp.concatenate([shift, scale, gate1, sums[0], sums[1], gate2[...]], axis=1)
    size = whole.shape[1] // tp
    clips = (da_o[0].shape[0] - own) // -(-size // width)
    for r in range(tp):
        value = whole[:, :size]
        for q in range(1, tp):
            here = lax.rem(rank[0] - r + tp, tp) == q
            value = jnp.where(here, whole[:, q * size : (q + 1) * size], value)
        for g in range(-(-size // width)):
            part = value[:, g * width : (g + 1) * width].astype(BF16)
            da_o[r][own + g * clips : own + (g + 1) * clips, : part.shape[1]] = part
        da_o[r].send()


def token_rows(tp, scalars, ins, outs):
    tok, g1, hot, mods, x2, live = ins[2 * tp :]
    both_o, cols_o = outs
    own, width = g1.shape
    n, inv = norm_parts(tok[:own].astype(F32))
    scale = 1.0 + expand(hot[:own], mods[1])
    gate = expand(hot[:own], mods[5])
    sums = total(ins[:tp])
    both_o[:own] = (g1[...] + norm_back(sums[:own] * scale, n, inv)).astype(BF16)
    both_o[own:] = ((x2[...] + gate * total(ins[tp : 2 * tp])) * live[:own]).astype(BF16)
    both_o.send()
    clips, size = cols_o.shape
    for g in range(-(-size // width)):
        at = own + g * clips
        part = sums[at : at + clips, : size - g * width]
        cols_o[:, g * width : g * width + part.shape[1]] = part


def place_rows(tp, scalars, ins, outs):
    (rank,) = scalars
    results, canon = outs[:-1], outs[-1]
    fmax, seqs = results[0].shape[:2]
    own_seqs = seqs // tp
    own = ins[0].shape[0] // 2
    for k in range(tp):
        canon[lax.rem(rank[0] - k + tp, tp)] = ins[k][...]
    for i, out in enumerate(results):
        for f in range(fmax):
            for q in range(tp):
                at = i * own + f * own_seqs
                out[f, q * own_seqs : (q + 1) * own_seqs] = canon[q, at : at + own_seqs]
        out.send()


def weight_grads(pairs, scalars, ins, outs):
    out = outs[0].bufs[0]
    refs = [item.ref() for item in ins]
    step = math.gcd(out.shape[0], 128)
    filled = sum(refs[2 * j + 1].shape[1] for j in range(pairs))
    if filled < out.shape[1]:
        out[:, filled:] = jnp.zeros((out.shape[0], out.shape[1] - filled), BF16)

    def some(i, carry):
        at = pl.ds(pl.multiple_of(i * step, step), step)
        start = 0
        for j in range(pairs):
            left, right = refs[2 * j], refs[2 * j + 1]
            width = right.shape[1]
            out[at, start : start + width] = dot_tn(left[:, at], right[...]).astype(BF16)
            start += width
        return carry

    lax.fori_loop(0, out.shape[0] // step, some, 0)


def finish_mlp(scalars, ins, outs):
    up_o, down_o = outs
    hid = up_o.shape[1]
    value = total(ins)
    up_o[...] = value[:, :hid]
    up_o.send()
    down_o[...] = value[:, hid:]


def caption_chunks(tp, scalars, ins, outs):
    (rank,) = scalars
    w_kv, d_kv = ins
    feats = outs[0].shape[1]
    w_kv[:8]
    for r, out in enumerate(outs):
        block = lax.rem(rank[0] - r + tp, tp)
        at = pl.ds(pl.multiple_of(block * feats, 8), feats)
        out[...] = dot_nt(d_kv[...], w_kv[at, :]).astype(BF16)
        out.send()


def finish_rest(scalars, ins, outs):
    (value,) = ins
    q2_o, kv2_o, out2_o, qkv_o, out_o = outs
    inner = q2_o.shape[1]
    half = value.shape[1] // 2

    def part(i):
        at = (i // 4) * half + (i % 4) * inner
        return value[:, at : at + inner].astype(F32)

    q2_o[...] = part(0)
    q2_o.send()
    for i in range(2):
        kv2_o[:, i, :] = part(1 + i)
    kv2_o.send()
    out2_o[...] = part(3)
    out2_o.send()
    for i in range(3):
        qkv_o[i] = part(4 + i)
    qkv_o.send()
    out_o[...] = part(7)


def join_rows(keys, clips, scalars, ins, outs):
    (out_o,) = outs
    value = total(ins)
    half = value.shape[1] // 2
    out_o[...] = value.astype(BF16)
    cond = value[keys : keys + clips, :half] + value[keys : keys + clips, half:]
    high = cond.astype(BF16)
    out_o[keys : keys + clips, :half] = high
    out_o[keys : keys + clips, half:] = (cond - high.astype(F32)).astype(BF16)


def place_captions(clips, scalars, ins, outs):
    (cap_len,) = scalars
    parts, condition = ins
    out_o, cond_o, rows = outs
    slots = out_o.shape[2]
    keys, feats = rows.shape
    blocks = parts.shape[0]
    size = keys // blocks
    half = cond_o.shape[1] // blocks
    wide = parts.shape[2] // 2
    conds = []
    for m in range(blocks):
        rows[m * size : (m + 1) * size] = parts[m, :size, :feats]
        value = parts[m, size : size + clips].astype(F32)
        conds.append(value[:, :half] + value[:, wide : wide + half])
    value = condition[...]
    sig = jax.nn.sigmoid(value)
    cond_o[...] = jnp.concatenate(conds, axis=1) * (sig + value * sig * (1.0 - sig))
    cond_o.send()
    slot = lax.broadcasted_iota(jnp.int32, (keys, slots), 1)
    key = lax.broadcasted_iota(jnp.int32, (keys, slots), 0)
    target = out_o.bufs[0]

    def some(c, start):
        pick = (slot + start == key) & (slot < cap_len[c])
        target[c] = dot_tn(rows[...], jnp.where(pick, 1.0, 0.0).astype(BF16))
        return start + cap_len[c]

    lax.fori_loop(0, clips, some, jnp.int32(0))


def ada_grads(scalars, ins, outs):
    mod_cols, scaled, w_ada = ins
    grad_o, cond_o = outs
    high = mod_cols[...].astype(BF16)
    low = (mod_cols[...] - high.astype(F32)).astype(BF16)
    grad_o[...] = dot_tn(scaled[...], high) + dot_tn(scaled[...], low)
    grad_o.send()
    cond = split_dot(dot_nt, mod_cols[...], w_ada[...])
    top = cond.astype(BF16)
    half = cond_o.shape[1] // 2
    cond_o[...] = jnp.zeros(cond_o.shape, BF16)
    cond_o[:, : cond.shape[1]] = top
    cond_o[:, half : half + cond.shape[1]] = (cond - top.astype(F32)).astype(BF16)


def after(value, *first):
    return lax.optimization_barrier((value,) + first)[0]


def tp_gather(value, tp):
    return [value] + [
        lax.ppermute(value, "tp", [(i, (i + k) % tp) for i in range(tp)]) for k in range(1, tp)
    ]


def tp_scatter(chunks, tp):
    return [chunks[0]] + [
        lax.ppermute(chunks[r], "tp", [(i, (i - r) % tp) for i in range(tp)]) for r in range(1, tp)
    ]


def seq_xor(value, mask, nseq):
    return lax.ppermute(value, "seq", [(i, i ^ mask) for i in range(nseq)])


def seq_total(value, nseq):
    mask = 1
    while mask < nseq:
        value = value + seq_xor(value, mask, nseq)
        mask *= 2
    return value


def far_gather(value, nseq):
    return [value] + [seq_xor(value, m, nseq) for m in range(2, nseq, 2)]


def near_gather(far, nseq):
    pieces = []
    for value in far:
        pieces += [value, seq_xor(value, 1, nseq)]
    return pieces


def padded(value, size, axis):
    if value.shape[axis] == size:
        return value
    pads = [(0, 0)] * value.ndim
    pads[axis] = (0, size - value.shape[axis])
    return jnp.pad(value, pads)


def shards(
    tokens,
    cotangent,
    caption,
    condition,
    frames,
    cap_len,
    clip_of,
    w_qkv,
    w_out,
    w_query2,
    w_kv2,
    w_out2,
    w_up,
    w_down,
    w_ada,
):
    tp, nseq = lax.axis_size("tp"), lax.axis_size("seq")
    me, spot = lax.axis_index("tp"), lax.axis_index("seq")
    seqs, fmax, width = tokens.shape
    clips, slots = caption.shape[:2]
    inner, hid = w_query2.shape[1], w_up.shape[1]
    heads = inner // HDIM
    drows = w_query2.shape[0]
    own_seqs = seqs // tp
    own = -(-own_seqs * fmax // 8) * 8
    rows = tp * own
    clip_pad = 8
    keys = -(-(clips * slots // 2) // 128) * 128
    mod_size = 6 * width // tp
    rank = jnp.stack([me, spot]).astype(jnp.int32)
    part = functools.partial

    tok, g3, hot, row_clip, row_id, key_id, live, turned = call(
        part(prepare_rows, tp),
        [
            sds((rows, width)),
            sds((rows, width)),
            sds((rows, clip_pad)),
            sds((rows, 1), jnp.int32),
            sds((rows, 1), jnp.int32),
            sds((1, rows), jnp.int32),
            sds((rows, 1), F32),
            sds((clip_pad, rows)),
        ],
        [tokens.transpose(1, 0, 2), cotangent.transpose(1, 0, 2)],
        work=[sds((tp, own, width))],
        smem=[rank, clip_of, frames],
        name="prepare_rows",
    )
    cap, key_clip = call(
        live_captions,
        [sds((keys, width)), sds((1, keys), jnp.int32)],
        [caption],
        smem=[cap_len],
        name="live_captions",
    )
    lane = lambda n: -(-n // 128) * 128
    section = jnp.concatenate(
        [padded(w_query2, lane(inner), 1), w_kv2.reshape(drows, 2 * inner)], axis=1
    )
    full_b = lax.all_gather(section, "seq", axis=0, tiled=True)
    pack_a = jnp.concatenate([w_qkv.reshape(drows, 3 * inner), w_out.T], axis=1)
    scaled = jax.nn.silu(condition).astype(BF16)
    scaled_own = lax.dynamic_slice_in_dim(scaled, spot * drows, drows, 1)
    mod_part = jnp.dot(scaled_own, w_ada, preferred_element_type=F32)
    mod_part = seq_total(mod_part, nseq)
    far_a = far_gather(after(pack_a, mod_part), nseq)
    z_pack = jnp.concatenate([w_query2, w_out2.T], axis=1)
    groups = mod_size // (2 * inner)
    high = lax.reduce_precision(mod_part, 8, 7)
    mod_rows = [
        part_[:, g * 2 * inner : (g + 1) * 2 * inner].astype(BF16)
        for part_ in (high, mod_part - high)
        for g in range(groups)
    ]
    z_rest = tp_gather(jnp.concatenate([z_pack] + mod_rows, axis=0), tp)
    z_rest = lax.optimization_barrier((*z_rest, tok, cap, *far_a[1:]))[:tp]
    (mods,) = call(
        part(modulations, tp, clips, drows),
        [sds((6, clip_pad, width), F32)],
        [Near(p) for p in z_rest],
        smem=[rank],
        name="modulations",
    )
    z_q2 = [p[:drows, :inner] for p in z_rest[1:]]
    z_out2 = [p[:drows, inner:] for p in z_rest]
    pack_c = jnp.concatenate(
        z_out2 + [padded(w_up, lane(hid), 1), padded(w_down.T, lane(hid), 1)], axis=1
    )
    full_c = lax.all_gather(pack_c, "seq", axis=0, tiled=True)
    full_d = lax.all_gather(jnp.concatenate(z_q2, axis=1), "seq", axis=0, tiled=True)
    w_q2 = Cols(full_b, 0, lane(inner))
    w_kv = Cols(full_b, lane(inner), 2 * inner)
    w_d = Cols(full_d, 0, full_d.shape[1])

    w_a = Blocks(near_gather(far_a, nseq))

    outs = call(
        part(frame_forward, tp),
        [
            sds((rows, width)),
            sds((rows, 3 * inner)),
            sds((heads, rows, rows)),
            sds((rows, inner)),
        ]
        + [sds((own, width))] * tp,
        [tok, hot, mods, row_id, key_id, w_a],
        smem=[rank],
        work=[sds((3, heads, rows, HDIM)), sds((heads, rows, HDIM))],
        name="frame_forward",
    )
    attn_in, qkv, probs, frame_out = outs[:4]
    branch_parts = tp_scatter(outs[4:], tp)
    x1_own, low_own, own_b1 = call(
        part(first_rows, tp),
        [sds((own, width), F32), sds((own, width)), sds((own, width), F32)],
        [*far(branch_parts), tok, hot, mods],
        name="first_rows",
    )
    low_parts = tp_gather(low_own, tp)
    (kv,) = call(
        key_values,
        [sds((keys, 2 * inner))],
        [cap, w_kv],
        name="key_values",
    )
    first_low, cq, cprobs, cross_out, cross_pack = call(
        part(cross_forward, tp, inner),
        [
            sds((rows, width)),
            sds((rows, inner)),
            sds((heads, rows, keys)),
            sds((rows, inner)),
            sds((own, tp * inner)),
        ],
        [*far(low_parts), row_clip, key_clip, w_q2, kv],
        work=[
            sds((heads, rows, HDIM)),
            sds((2, heads, keys, HDIM)),
            sds((heads, rows, HDIM)),
        ],
        name="cross_forward",
    )
    cross_parts = tp_gather(cross_pack, tp)
    outs = call(
        part(mlp_both, tp, inner),
        [
            sds((own, width), F32),
            sds((rows, width)),
            sds((rows, hid)),
            sds((rows, width)),
            sds((rows, hid)),
        ]
        + [sds((clip_pad, width), F32)]
        + [sds((own, width))] * (2 * tp),
        [
            *far(cross_parts),
            x1_own,
            first_low,
            g3,
            hot,
            mods,
            Cols(full_c, 0, width),
            Cols(full_c, width, lane(hid)),
            Cols(full_c, width + lane(hid), lane(hid)),
            turned,
        ],
        smem=[rank],
        name="mlp_both",
    )
    x2_own, mlp_in, hidden, d_b3, d_pre = outs[:5]
    sum_gate2 = outs[5]
    dm_chunks, b3_chunks = outs[6 : 6 + tp], outs[6 + tp :]

    dm_parts = tp_scatter(dm_chunks, tp)
    (grad_one,) = call(
        part(weight_grads, 2),
        [sds((width, 2 * hid))],
        [mlp_in, d_pre, d_b3, hidden],
        name="grads_mlp",
    )
    g2_own, db2_own, sums_two = call(
        part(second_back, tp),
        [sds((own, width), F32), sds((own, width)), sds((2, clip_pad, width), F32)],
        [*far(dm_parts), x2_own, g3, hot, mods, turned],
        order=[grad_one],
        name="second_back",
    )
    sum_one = lax.psum_scatter(after(grad_one, db2_own), "seq", scatter_dimension=0, tiled=True)
    db2_parts = tp_gather(db2_own, tp)
    d_b2, d_cq, d_kv, dcq_pack, kv_rel = call(
        part(cross_back, tp, inner),
        [
            sds((rows, width)),
            sds((rows, inner)),
            sds((keys, 2 * inner)),
            sds((own, tp * inner)),
            sds((nseq, keys // nseq, 2 * inner)),
        ],
        [*far(db2_parts), Cols(full_c, 0, lane(inner)), cprobs, kv, cq],
        work=[
            sds((heads, rows, HDIM)),
            sds((2, heads, keys, HDIM)),
            sds((heads, rows, HDIM)),
            sds((heads, rows, HDIM)),
            sds((heads, rows, keys)),
            sds((2, heads, keys, HDIM)),
        ],
        smem=[rank],
        name="cross_back",
    )
    dcq_parts = tp_gather(dcq_pack, tp)
    (grad_two,) = call(
        part(weight_grads, 3),
        [Half((width, 2 * lane(4 * inner)), 0, lane(4 * inner))],
        [first_low, d_cq, cap, d_kv, d_b2, cross_out],
        name="grads_cross",
    )
    half = nseq // 2
    kv_away = seq_xor(kv_rel[half:], 1, nseq)
    kv_sums = (kv_rel[:half].astype(F32) + kv_away.astype(F32)).astype(BF16)
    kv_own = kv_sums[0].astype(F32)
    for c in range(1, half):
        kv_own = kv_own + seq_xor(kv_sums[c], 2 * c, nseq).astype(F32)
    kv_own = kv_own.astype(BF16)
    outs = call(
        part(frame_back, tp, inner),
        [sds((own, width), F32), sds((rows, width)), sds((rows, 3 * inner))]
        + [sds((own + clip_pad * -(-mod_size // width), width))] * tp,
        [
            *far(dcq_parts),
            d_b2,
            g2_own,
            hot,
            mods,
            w_q2,
            w_d,
            w_a,
            qkv,
            probs,
            tok,
            own_b1,
            sums_two,
            sum_gate2,
            turned,
        ],
        smem=[rank],
        order=[Near(kv_sums)],
        work=[
            sds((3, heads, rows, HDIM)),
            sds((heads, rows, HDIM)),
            sds((3, heads, rows, HDIM)),
            sds((rows, width)),
            sds((rows, width), F32),
            sds((3, clip_pad, width), F32),
        ],
        name="frame_back",
    )
    g1_own, d_b1, d_qkv = outs[:3]
    da_chunks = outs[3:]
    b3_parts = tp_scatter([after(b, grad_two, *dcq_parts[1:]) for b in b3_chunks], tp)
    da_parts = tp_scatter([after(d, *b3_parts[1:]) for d in da_chunks], tp)
    (grad_three,) = call(
        part(weight_grads, 2),
        [Half((width, 2 * lane(4 * inner)), lane(4 * inner), lane(4 * inner))],
        [attn_in, d_qkv, d_b1, frame_out],
        order=[grad_two],
        keep=True,
        name="grads_frame",
    )
    sum_rest = lax.psum_scatter(
        after(grad_three, *da_parts[1:]), "seq", scatter_dimension=0, tiled=True
    )
    grad_up, grad_down = call(
        finish_mlp,
        [sds((drows, hid), F32), sds((drows, hid), F32)],
        [sum_one],
        name="finish_mlp",
    )
    feats = width // tp
    cap_chunks = call(
        part(caption_chunks, tp),
        [sds((keys // nseq, feats))] * tp,
        [w_kv, Near(kv_own)],
        smem=[rank],
        name="caption_chunks",
    )
    both_own, mod_cols = call(
        part(token_rows, tp),
        [sds((2 * own, width)), sds((clip_pad, mod_size), F32)],
        [*far(da_parts), *far(b3_parts), tok, g1_own, hot, mods, x2_own, live],
        order=[grad_three, grad_up, cap_chunks[0]],
        name="token_rows",
    )
    both_parts = tp_gather(both_own, tp)
    mod_cols = seq_total(mod_cols, nseq)

    span = max(feats, 2 * drows)
    grad_ada, cond_rows = call(
        ada_grads,
        [sds(w_ada.shape, F32), sds((clip_pad, span))],
        [Near(mod_cols), Near(padded(scaled_own, clip_pad, 0)), w_ada],
        name="ada_grads",
    )
    shared = [jnp.concatenate([padded(c, span, 1), cond_rows], axis=0) for c in cap_chunks]
    shared = tp_scatter([after(c, *both_parts[1:]) for c in shared], tp)
    (block,) = call(
        part(join_rows, keys // nseq, clips),
        [sds((keys // nseq + clip_pad, span))],
        far(shared),
        name="join_rows",
    )
    blocks = lax.all_gather(block, "seq", axis=0)
    d_tokens, output = call(
        part(place_rows, tp),
        [sds((fmax, seqs, width))] * 2,
        far(both_parts),
        work=[sds((tp, 2 * own, width))],
        smem=[rank],
        name="place_rows",
    )

    d_caption, d_condition = call(
        part(place_captions, clips),
        [sds((clips, feats, slots), F32), sds((clips, width), F32)],
        [Near(blocks), condition],
        work=[sds((keys, feats))],
        smem=[cap_len],
        order=[output, grad_ada],
        name="place_captions",
    )

    grad_q2, grad_kv2, grad_out2, grad_qkv, grad_out = call(
        finish_rest,
        [
            sds((drows, inner), F32),
            sds((drows, 2, inner), F32),
            sds((drows, inner), F32),
            sds((3, drows, inner), F32),
            sds((drows, inner), F32),
        ],
        [sum_rest],
        order=[d_caption],
        name="finish_rest",
    )

    return (
        output.transpose(1, 0, 2),
        d_tokens.transpose(1, 0, 2),
        d_caption.transpose(0, 2, 1),
        d_condition,
        grad_qkv.transpose(1, 0, 2),
        grad_out.T,
        grad_q2,
        grad_kv2,
        grad_out2.T,
        grad_up,
        grad_down.T,
        grad_ada,
    )


def solution(mesh):
    return jax.shard_map(
        shards,
        mesh=mesh,
        in_specs=(
            P("seq", None, None),
            P("seq", None, None),
            P(),
            P(),
            P(),
            P(),
            P("seq"),
            P("seq", None, "tp"),
            P("tp", "seq"),
            P("seq", "tp"),
            P("seq", None, "tp"),
            P("tp", "seq"),
            P("seq", "tp"),
            P("tp", "seq"),
            P("seq", "tp"),
        ),
        out_specs=(
            P("seq", None, None),
            P("seq", None, None),
            P(None, None, "tp"),
            P(),
            P("seq", None, "tp"),
            P("tp", "seq"),
            P("seq", "tp"),
            P("seq", None, "tp"),
            P("tp", "seq"),
            P("seq", "tp"),
            P("tp", "seq"),
            P("seq", "tp"),
        ),
        check_vma=False,
    )
```

profile of v0, /device:TPU:0, one launch (start us, length us, event | category | flops | bytes accessed | tf_op | source)
XLA Modules:
  0.0 333.3 jit_solution(6722908584238526152)
XLA Ops:
  37.1 7.6 %live_captions.1 = (bf16[640,1152]{1,0:T(8,128)(2,1)}, s32[1,640]{1,0:T(1,128)}) custom-call(s32[4]{0:T(128)S(1)} %copy-done, bf16[4,300,1152]{2,1,0:T(8,128)(2,1)} %copy.30.refs_1_), custom_call_target="tpu_custom_call" | custom-call | bytes 4241920 | tf_op jit(solution)/shard_map/live_captions/pallas_call | solution.py:180
  56.3 8.9 %frame_forward.1 = (bf16[288,1152]{1,0:T(8,128)(2,1)}, bf16[288,864]{1,0:T(8,128)(2,1)}, bf16[4,288,288]{2,1,0:T(8,128)(2,1)}, bf16[288,288]{1,0:T(8,128)(2,1)},...) custom-call(s32[2]{0:T(128)S(1)} %pad_add_fusion.refs_0_, ...), custom_call_target="tpu_custom_call" | custom-call | bytes 6200064 | tf_op jit(solution)/shard_map/frame_forward/pallas_call | solution.py:180
  65.3 9.8 %collective-permute-start.13 = (bf16[72,1152]{1,0:T(8,128)(2,1)}, bf16[72,1152]{1,0:T(8,128)(2,1)S(1)}, u32[]{:S(2)}, u32[]{:S(2)}) collective-permute-start(bf16[72,1152]{1,0:T(8,128)(2,1)} %get-tuple-element.116), channel_id=1, source_target_pairs={{0,3},{1,0},{2,1},{3,2},{4,7},{5,4},{6,5},{7,6},{8,11},{9,8},{10,9... | collective-permute-start | bytes 497672 | tf_op jit(solution)/shard_map/ppermute | solution.py:855
  75.7 4.4 %collective-permute-done.13.refs_1_ = bf16[72,1152]{1,0:T(8,128)(2,1)S(1)} collective-permute-done((bf16[72,1152]{1,0:T(8,128)(2,1)}, bf16[72,1152]{1,0:T(8,128)(2,1)S(1)}, u32[]{:S(2)}, u32[]{:S(2)}) %collective-permute-start.13) | collective-permute-done | bytes 165920 | tf_op jit(solution)/shard_map/ppermute | solution.py:855
  80.1 9.2 %collective-permute-done.14.refs_2_ = bf16[72,1152]{1,0:T(8,128)(2,1)S(1)} collective-permute-done((bf16[72,1152]{1,0:T(8,128)(2,1)}, bf16[72,1152]{1,0:T(8,128)(2,1)S(1)}, u32[]{:S(2)}, u32[]{:S(2)}) %collective-permute-start.14) | collective-permute-done | bytes 165920 | tf_op jit(solution)/shard_map/ppermute | solution.py:855
  97.8 5.0 %key_values.1.refs_7_ = bf16[640,576]{1,0:T(8,128)(2,1)} custom-call(bf16[640,1152]{1,0:T(8,128)(2,1)} %get-tuple-element.107.refs_0_.refs_2_, bf16[1152,960]{1,0:T(8,128)(2,1)} %all-gather.5.cloned.1.call-done.refs_1_.refs_6_.refs_9_), custom_call_target="tpu_custom_call" | custom-call | bytes 4423680 | tf_op jit(solution)/shard_map/key_values/pallas_call | solution.py:180
  106.6 7.7 %cross_forward.1 = (bf16[288,1152]{1,0:T(8,128)(2,1)}, bf16[288,288]{1,0:T(8,128)(2,1)}, bf16[4,288,640]{2,1,0:T(8,128)(2,1)}, bf16[288,288]{1,0:T(8,128)(2,1)}, bf16[72,1152]{1,0:T(8,128)(2,1)}) custom-call(bf16[72,1152]{1,0:T(8,128)(2,1)} %get-tuple-element.119.refs_0_, bf16[72,1152]{1,0:T(8,128)(2,1)S(1)} %collective-permute-done.16.refs_1_, ...), custom_call_target="tpu_custom_call" | custom-call | bytes 6252160 | tf_op jit(solution)/shard_map/cross_forward/pallas_call | solution.py:180
  120.8 4.5 %collective-permute-done.19.refs_2_ = bf16[72,1152]{1,0:T(8,128)(2,1)S(1)} collective-permute-done((bf16[72,1152]{1,0:T(8,128)(2,1)}, bf16[72,1152]{1,0:T(8,128)(2,1)S(1)}, u32[]{:S(2)}, u32[]{:S(2)}) %collective-permute-start.19) | collective-permute-done | bytes 165920 | tf_op jit(solution)/shard_map/ppermute | solution.py:849
  125.2 5.3 %collective-permute-done.20.refs_3_ = bf16[72,1152]{1,0:T(8,128)(2,1)S(1)} collective-permute-done((bf16[72,1152]{1,0:T(8,128)(2,1)}, bf16[72,1152]{1,0:T(8,128)(2,1)S(1)}, u32[]{:S(2)}, u32[]{:S(2)}) %collective-permute-start.20) | collective-permute-done | bytes 165920 | tf_op jit(solution)/shard_map/ppermute | solution.py:849
  130.6 12.9 %mlp_both.1 = (f32[72,1152]{1,0:T(8,128)}, bf16[288,1152]{1,0:T(8,128)(2,1)}, bf16[288,1152]{1,0:T(8,128)(2,1)}, bf16[288,1152]{1,0:T(8,128)(2,1)}, bf16[288,115...) custom-call(s32[2]{0:T(128)S(1)} %pad_add_fusion.refs_0_, ...), custom_call_target="tpu_custom_call" | custom-call | bytes 30790656 | tf_op jit(solution)/shard_map/mlp_both/pallas_call | solution.py:180
  143.5 5.8 %collective-permute-start.22 = (bf16[72,1152]{1,0:T(8,128)(2,1)}, bf16[72,1152]{1,0:T(8,128)(2,1)S(1)}, u32[]{:S(2)}, u32[]{:S(2)}) collective-permute-start(bf16[72,1152]{1,0:T(8,128)(2,1)} %get-tuple-element.128), channel_id=1, source_target_pairs={{0,3},{1,0},{2,1},{3,2},{4,7},{5,4},{6,5},{7,6},{8,11},{9,8},{10,9... | collective-permute-start | bytes 497672 | tf_op jit(solution)/shard_map/ppermute | solution.py:855
  150.0 8.9 %grads_mlp.1.refs_9_ = bf16[1152,2304]{1,0:T(8,128)(2,1)} custom-call(bf16[288,1152]{1,0:T(8,128)(2,1)} %get-tuple-element.132.refs_0_, bf16[288,1152]{1,0:T(8,128)(2,1)} %get-tuple-element.133.refs_1_, bf16[288,1152]{1,0:T(8,128)(2,1)} %get-tuple-element.134.refs_2_, bf16[288,1152]{1,0:T(8,128)(2,1)} %get-tuple-element.135.refs_3_), custom_call_target="tpu_custom_call" | custom-call | bytes 7962624 | tf_op jit(solution)/shard_map/grads_mlp/pallas_call | solution.py:180
  158.9 5.2 %collective-permute-done.23.refs_2_ = bf16[72,1152]{1,0:T(8,128)(2,1)S(1)} collective-permute-done((bf16[72,1152]{1,0:T(8,128)(2,1)}, bf16[72,1152]{1,0:T(8,128)(2,1)S(1)}, u32[]{:S(2)}, u32[]{:S(2)}) %collective-permute-start.23) | collective-permute-done | bytes 165920 | tf_op jit(solution)/shard_map/ppermute | solution.py:855
  172.6 4.3 %collective-permute-done.25.refs_2_ = bf16[72,1152]{1,0:T(8,128)(2,1)S(1)} collective-permute-done((bf16[72,1152]{1,0:T(8,128)(2,1)S(1)}, bf16[72,1152]{1,0:T(8,128)(2,1)S(1)}, u32[]{:S(2)}, u32[]{:S(2)}) %collective-permute-start.25) | collective-permute-done | bytes 165920 | tf_op jit(solution)/shard_map/ppermute | solution.py:849
  176.9 5.4 %collective-permute-done.26.refs_3_ = bf16[72,1152]{1,0:T(8,128)(2,1)S(1)} collective-permute-done((bf16[72,1152]{1,0:T(8,128)(2,1)S(1)}, bf16[72,1152]{1,0:T(8,128)(2,1)S(1)}, u32[]{:S(2)}, u32[]{:S(2)}) %collective-permute-start.26) | collective-permute-done | bytes 165920 | tf_op jit(solution)/shard_map/ppermute | solution.py:849
  182.3 10.1 %cross_back.1 = (bf16[288,1152]{1,0:T(8,128)(2,1)}, bf16[288,288]{1,0:T(8,128)(2,1)}, bf16[640,576]{1,0:T(8,128)(2,1)}, bf16[72,1152]{1,0:T(8,128)(2,1)}, bf16[8,80,576]{2,1,0:T(8,128)(2,1)}) custom-call(s32[2]{0:T(128)S(1)} %pad_add_fusion.refs_0_, bf16[72,1152]{1,0:T(8,128)(2,1)} %get-tuple-element.136.refs_1_, ...), custom_call_target="tpu_custom_call" | custom-call | bytes 13473792 | tf_op jit(solution)/shard_map/cross_back/pallas_call | solution.py:180
  199.2 8.9 %grads_cross.1 = bf16[1152,2304]{1,0:T(8,128)(2,1)} custom-call(bf16[288,1152]{1,0:T(8,128)(2,1)} %get-tuple-element.124.refs_6_.refs_0_, bf16[288,288]{1,0:T(8,128)(2,1)} %get-tuple-element.150.refs_1_, bf16[640,1152]{1,0:T(8,128)(2,1)} %get-tuple-element.107.refs_0_.refs_2_, bf16[640,576]{1,0:T(8,128)(2,1)} %get-tuple-element.151.refs_3_, ...), custom_call_target="tpu_custom_call" | custom-call | bytes 9179136 | tf_op jit(solution)/shard_map/grads_cross/pallas_call | solution.py:180
  210.1 4.7 %collective-permute-start.32 = (bf16[72,1152]{1,0:T(8,128)(2,1)S(1)}, bf16[72,1152]{1,0:T(8,128)(2,1)S(1)}, u32[]{:S(2)}, u32[]{:S(2)}) collective-permute-start(bf16[72,1152]{1,0:T(8,128)(2,1)S(1)} %copy-done.21), channel_id=1, source_target_pairs={{0,3},{1,0},{2,1},{3,2},{4,7},{5,4},{6,5},{7,6},{8,11},{9,8},{10,9... | collective-permute-start | bytes 497672 | tf_op jit(solution)/shard_map/ppermute | solution.py:855
  215.8 13.7 %frame_back.1 = (f32[72,1152]{1,0:T(8,128)}, bf16[288,1152]{1,0:T(8,128)(2,1)}, bf16[288,864]{1,0:T(8,128)(2,1)}, bf16[88,1152]{1,0:T(8,128)(2,1)}, bf16[88,1152...) custom-call(s32[2]{0:T(128)S(1)} %pad_add_fusion.refs_0_, ...), custom_call_target="tpu_custom_call" | custom-call | bytes 13317120 | tf_op jit(solution)/shard_map/frame_back/pallas_call | solution.py:180
  236.4 7.4 %grads_frame.1.refs_14_ = bf16[1152,2304]{1,0:T(8,128)(2,1)} custom-call(bf16[288,1152]{1,0:T(8,128)(2,1)} %get-tuple-element.169.refs_0_, bf16[288,864]{1,0:T(8,128)(2,1)} %get-tuple-element.170.refs_1_, bf16[288,1152]{1,0:T(8,128)(2,1)} %get-tuple-element.171.refs_2_, bf16[288,288]{1,0:T(8,128)(2,1)} %get-tuple-element.172.refs_3_, ...), custom_call_target="tpu_custom_call", output_to_operand_aliasing={{}: (4, {})} | custom-call | bytes 7299072 | tf_op jit(solution)/shard_map/grads_frame/pallas_call | solution.py:180
  243.8 7.1 %collective-permute-done.36.refs_2_ = bf16[88,1152]{1,0:T(8,128)(2,1)S(1)} collective-permute-done((bf16[88,1152]{1,0:T(8,128)(2,1)}, bf16[88,1152]{1,0:T(8,128)(2,1)S(1)}, u32[]{:S(2)}, u32[]{:S(2)}) %collective-permute-start.36) | collective-permute-done | bytes 202784 | tf_op jit(solution)/shard_map/ppermute | solution.py:855
  292.0 9.9 %collective-permute-start.47 = (bf16[88,288]{1,0:T(8,128)(2,1)S(1)}, bf16[88,288]{1,0:T(8,128)(2,1)S(1)}, u32[]{:S(2)}, u32[]{:S(2)}) collective-permute-start(bf16[88,288]{1,0:T(8,128)(2,1)S(1)} %get-tuple-element.183), channel_id=1, source_target_pairs={{0,3},{1,0},{2,1},{3,2},{4,7},{5,4},{6,5},{7,6},{8,11},{9,8},{10,9... | collective-permute-start | bytes 152072 | tf_op jit(solution)/shard_map/ppermute | solution.py:855
  309.6 10.1 %all-gather = bf16[704,288]{1,0:T(8,128)(2,1)S(1)} all-gather(bf16[88,288]{1,0:T(8,128)(2,1)} %join_rows.1), channel_id=2, replica_groups=mesh['seq'=8,'tp'=4] {'seq'}, dimensions={0}, use_global_device_ids=true | all-gather | bytes 456192 | tf_op jit(solution)/shard_map/all_gather | solution.py:1203
  319.7 4.3 %place_captions.1 = (f32[4,288,300]{2,1,0:T(8,128)}, f32[4,1152]{1,0:T(4,128)}) custom-call(s32[4]{0:T(128)S(1)} %copy-done, bf16[8,88,288]{2,1,0:T(8,128)(2,1)S(1)} %bitcast.28, f32[4,1152]{1,0:T(4,128)} %refs_2_.5, bf16[17,16,1152]{2,1,0:T(8,128)(2,1)} %get-tuple-element.177.refs_3_, f32[144,1728]{1,0:T(8,128)} %get-tuple-element.104.refs_4_), custom_call_target="tpu_custom_call" | custom-call | bytes 1824768 | tf_op jit(solution)/shard_map/place_captions/pallas_call | solution.py:180
  (195 shorter events, 137.7 us)
Async XLA Ops:
  7.2 90.6 %all-gather.5.cloned.1.call-start = ((), (), s32[]{:S(2)}) async-start(), calls=%async_computation.2 | async-start | bytes 2654208 | tf_op jit(solution)/shard_map/all_gather | solution.py:951
  10.0 120.6 %all-gather.7.cloned.1.call-start = ((), (), s32[]{:S(2)}) async-start(), calls=%async_computation.3 | async-start | bytes 8957952 | tf_op jit(solution)/shard_map/all_gather | solution.py:980
  24.9 23.1 %collective-permute-start.6 = (bf16[144,1152]{1,0:T(8,128)(2,1)S(1)}, bf16[144,1152]{1,0:T(8,128)(2,1)S(1)}, u32[]{:S(2)}, u32[]{:S(2)}) collective-permute-start(bf16[144,1152]{1,0:T(8,128)(2,1)S(1)} %pad_maximum_fusion.refs_6_.refs_11_), channel_id=1, source_target_pairs={{0,8},{4,12},{8,0},{12,4},{16,24},{20,28},{24,16},{28,20},{1,9},{5... | collective-permute-start | bytes 995336 | tf_op jit(solution)/shard_map/ppermute | solution.py:860
  26.5 21.6 %collective-permute-start.7 = (bf16[144,1152]{1,0:T(8,128)(2,1)S(1)}, bf16[144,1152]{1,0:T(8,128)(2,1)S(1)}, u32[]{:S(2)}, u32[]{:S(2)}) collective-permute-start(bf16[144,1152]{1,0:T(8,128)(2,1)S(1)} %pad_maximum_fusion.refs_6_.refs_11_), channel_id=1, source_target_pairs={{0,16},{4,20},{8,24},{12,28},{16,0},{20,4},{24,8},{28,12},{1,17},{... | collective-permute-start | bytes 995336 | tf_op jit(solution)/shard_map/ppermute | solution.py:860
  28.3 19.8 %collective-permute-start.8 = (bf16[144,1152]{1,0:T(8,128)(2,1)S(1)}, bf16[144,1152]{1,0:T(8,128)(2,1)S(1)}, u32[]{:S(2)}, u32[]{:S(2)}) collective-permute-start(bf16[144,1152]{1,0:T(8,128)(2,1)S(1)} %pad_maximum_fusion.refs_6_.refs_11_), channel_id=1, source_target_pairs={{0,24},{4,28},{8,16},{12,20},{16,8},{20,12},{24,0},{28,4},{1,25},{... | collective-permute-start | bytes 995336 | tf_op jit(solution)/shard_map/ppermute | solution.py:860
  28.5 19.5 %collective-permute-start.4 = (bf16[168,576]{1,0:T(8,128)(2,1)S(1)}, bf16[168,576]{1,0:T(8,128)(2,1)S(1)}, u32[]{:S(2)}, u32[]{:S(2)}) collective-permute-start(bf16[168,576]{1,0:T(8,128)(2,1)S(1)} %concatenate.31.refs_1_), channel_id=1, source_target_pairs={{0,2},{1,3},{2,0},{3,1},{4,6},{5,7},{6,4},{7,5},{8,10},{9,11},{10,... | collective-permute-start | bytes 580616 | tf_op jit(solution)/shard_map/ppermute | solution.py:849
  31.5 16.6 %collective-permute-start.5 = (bf16[168,576]{1,0:T(8,128)(2,1)S(1)}, bf16[168,576]{1,0:T(8,128)(2,1)S(1)}, u32[]{:S(2)}, u32[]{:S(2)}) collective-permute-start(bf16[168,576]{1,0:T(8,128)(2,1)S(1)} %concatenate.31.refs_1_), channel_id=1, source_target_pairs={{0,3},{1,0},{2,1},{3,2},{4,7},{5,4},{6,5},{7,6},{8,11},{9,8},{10,9... | collective-permute-start | bytes 580616 | tf_op jit(solution)/shard_map/ppermute | solution.py:849
  51.4 164.3 %all-gather.9.cloned.1.call-start = ((), (), s32[]{:S(2)}) async-start(), calls=%async_computation.4 | async-start | bytes 2322432 | tf_op jit(solution)/shard_map/all_gather | solution.py:981
  52.4 210.8 %reduce-scatter.3.cloned.1.call-start = ((), (), s32[]{:S(2)}) async-start(), calls=%async_computation.5 | async-start | bytes 5971968 | tf_op jit(solution)/shard_map/reduce_scatter | solution.py:1079
  65.3 14.8 %collective-permute-start.13 = (bf16[72,1152]{1,0:T(8,128)(2,1)}, bf16[72,1152]{1,0:T(8,128)(2,1)S(1)}, u32[]{:S(2)}, u32[]{:S(2)}) collective-permute-start(bf16[72,1152]{1,0:T(8,128)(2,1)} %get-tuple-element.116), channel_id=1, source_target_pairs={{0,3},{1,0},{2,1},{3,2},{4,7},{5,4},{6,5},{7,6},{8,11},{9,8},{10,9... | collective-permute-start | bytes 497672 | tf_op jit(solution)/shard_map/ppermute | solution.py:855
  143.5 15.4 %collective-permute-start.22 = (bf16[72,1152]{1,0:T(8,128)(2,1)}, bf16[72,1152]{1,0:T(8,128)(2,1)S(1)}, u32[]{:S(2)}, u32[]{:S(2)}) collective-permute-start(bf16[72,1152]{1,0:T(8,128)(2,1)} %get-tuple-element.128), channel_id=1, source_target_pairs={{0,3},{1,0},{2,1},{3,2},{4,7},{5,4},{6,5},{7,6},{8,11},{9,8},{10,9... | collective-permute-start | bytes 497672 | tf_op jit(solution)/shard_map/ppermute | solution.py:855
  149.3 14.8 %collective-permute-start.23 = (bf16[72,1152]{1,0:T(8,128)(2,1)}, bf16[72,1152]{1,0:T(8,128)(2,1)S(1)}, u32[]{:S(2)}, u32[]{:S(2)}) collective-permute-start(bf16[72,1152]{1,0:T(8,128)(2,1)} %get-tuple-element.129), channel_id=1, source_target_pairs={{0,2},{1,3},{2,0},{3,1},{4,6},{5,7},{6,4},{7,5},{8,10},{9,11},{10,... | collective-permute-start | bytes 497672 | tf_op jit(solution)/shard_map/ppermute | solution.py:855
  149.3 14.8 %collective-permute-start.24 = (bf16[72,1152]{1,0:T(8,128)(2,1)}, bf16[72,1152]{1,0:T(8,128)(2,1)S(1)}, u32[]{:S(2)}, u32[]{:S(2)}) collective-permute-start(bf16[72,1152]{1,0:T(8,128)(2,1)} %get-tuple-element.130), channel_id=1, source_target_pairs={{0,1},{1,2},{2,3},{3,0},{4,5},{5,6},{6,7},{7,4},{8,9},{9,10},{10,1... | collective-permute-start | bytes 497672 | tf_op jit(solution)/shard_map/ppermute | solution.py:855
  167.0 157.0 %reduce-scatter.5.cloned.1.call-start = ((), (), s32[]{:S(2)}) async-start(), calls=%async_computation.6 | async-start | bytes 5971968 | tf_op jit(solution)/shard_map/reduce_scatter | solution.py:1161
  193.5 22.1 %collective-permute-start.31 = (bf16[4,80,576]{2,1,0:T(8,128)(2,1)S(1)}, bf16[4,80,576]{2,1,0:T(8,128)(2,1)S(1)}, u32[]{:S(2)}, u32[]{:S(2)}) collective-permute-start(bf16[4,80,576]{2,1,0:T(8,128)(2,1)S(1)} %slice.77), channel_id=1, source_target_pairs={{0,4},{4,0},{8,12},{12,8},{16,20},{20,16},{24,28},{28,24},{1,5},{5... | collective-permute-start | bytes 1105928 | tf_op jit(solution)/shard_map/ppermute | solution.py:860
  193.6 14.5 %collective-permute-start.28 = (bf16[72,1152]{1,0:T(8,128)(2,1)}, bf16[72,1152]{1,0:T(8,128)(2,1)S(1)}, u32[]{:S(2)}, u32[]{:S(2)}) collective-permute-start(bf16[72,1152]{1,0:T(8,128)(2,1)} %get-tuple-element.139.refs_1_), channel_id=1, source_target_pairs={{0,1},{1,2},{2,3},{3,0},{4,5},{5,6},{6,7},{7,4},{8,9},{9,10},{10,1... | collective-permute-start | bytes 497672 | tf_op jit(solution)/shard_map/ppermute | solution.py:849
  210.1 19.4 %collective-permute-start.32 = (bf16[72,1152]{1,0:T(8,128)(2,1)S(1)}, bf16[72,1152]{1,0:T(8,128)(2,1)S(1)}, u32[]{:S(2)}, u32[]{:S(2)}) collective-permute-start(bf16[72,1152]{1,0:T(8,128)(2,1)S(1)} %copy-done.21), channel_id=1, source_target_pairs={{0,3},{1,0},{2,1},{3,2},{4,7},{5,4},{6,5},{7,6},{8,11},{9,8},{10,9... | collective-permute-start | bytes 497672 | tf_op jit(solution)/shard_map/ppermute | solution.py:855
  214.8 15.6 %collective-permute-start.33 = (bf16[72,1152]{1,0:T(8,128)(2,1)S(1)}, bf16[72,1152]{1,0:T(8,128)(2,1)S(1)}, u32[]{:S(2)}, u32[]{:S(2)}) collective-permute-start(bf16[72,1152]{1,0:T(8,128)(2,1)S(1)} %copy-done.20), channel_id=1, source_target_pairs={{0,2},{1,3},{2,0},{3,1},{4,6},{5,7},{6,4},{7,5},{8,10},{9,11},{10,... | collective-permute-start | bytes 497672 | tf_op jit(solution)/shard_map/ppermute | solution.py:855
  215.6 14.8 %collective-permute-start.34 = (bf16[72,1152]{1,0:T(8,128)(2,1)S(1)}, bf16[72,1152]{1,0:T(8,128)(2,1)S(1)}, u32[]{:S(2)}, u32[]{:S(2)}) collective-permute-start(bf16[72,1152]{1,0:T(8,128)(2,1)S(1)} %copy-done.19), channel_id=1, source_target_pairs={{0,1},{1,2},{2,3},{3,0},{4,5},{5,6},{6,7},{7,4},{8,9},{9,10},{10,1... | collective-permute-start | bytes 497672 | tf_op jit(solution)/shard_map/ppermute | solution.py:855
  233.4 17.5 %collective-permute-start.36 = (bf16[88,1152]{1,0:T(8,128)(2,1)}, bf16[88,1152]{1,0:T(8,128)(2,1)S(1)}, u32[]{:S(2)}, u32[]{:S(2)}) collective-permute-start(bf16[88,1152]{1,0:T(8,128)(2,1)} %get-tuple-element.162), channel_id=1, source_target_pairs={{0,2},{1,3},{2,0},{3,1},{4,6},{5,7},{6,4},{7,5},{8,10},{9,11},{10,... | collective-permute-start | bytes 608264 | tf_op jit(solution)/shard_map/ppermute | solution.py:855
  233.8 17.1 %collective-permute-start.37 = (bf16[88,1152]{1,0:T(8,128)(2,1)}, bf16[88,1152]{1,0:T(8,128)(2,1)S(1)}, u32[]{:S(2)}, u32[]{:S(2)}) collective-permute-start(bf16[88,1152]{1,0:T(8,128)(2,1)} %get-tuple-element.164), channel_id=1, source_target_pairs={{0,1},{1,2},{2,3},{3,0},{4,5},{5,6},{6,7},{7,4},{8,9},{9,10},{10,1... | collective-permute-start | bytes 608264 | tf_op jit(solution)/shard_map/ppermute | solution.py:855
  268.9 22.2 %collective-permute-start.41 = (bf16[144,1152]{1,0:T(8,128)(2,1)}, bf16[144,1152]{1,0:T(8,128)(2,1)S(1)}, u32[]{:S(2)}, u32[]{:S(2)}) collective-permute-start(bf16[144,1152]{1,0:T(8,128)(2,1)} %get-tuple-element.176.refs_1_), channel_id=1, source_target_pairs={{0,1},{1,2},{2,3},{3,0},{4,5},{5,6},{6,7},{7,4},{8,9},{9,10},{10,1... | collective-permute-start | bytes 995336 | tf_op jit(solution)/shard_map/ppermute | solution.py:849
  269.0 22.9 %collective-permute-start.42 = (bf16[144,1152]{1,0:T(8,128)(2,1)}, bf16[144,1152]{1,0:T(8,128)(2,1)S(1)}, u32[]{:S(2)}, u32[]{:S(2)}) collective-permute-start(bf16[144,1152]{1,0:T(8,128)(2,1)} %get-tuple-element.176.refs_1_), channel_id=1, source_target_pairs={{0,2},{1,3},{2,0},{3,1},{4,6},{5,7},{6,4},{7,5},{8,10},{9,11},{10,... | collective-permute-start | bytes 995336 | tf_op jit(solution)/shard_map/ppermute | solution.py:849
  270.8 21.2 %collective-permute-start.43 = (bf16[144,1152]{1,0:T(8,128)(2,1)}, bf16[144,1152]{1,0:T(8,128)(2,1)S(1)}, u32[]{:S(2)}, u32[]{:S(2)}) collective-permute-start(bf16[144,1152]{1,0:T(8,128)(2,1)} %get-tuple-element.176.refs_1_), channel_id=1, source_target_pairs={{0,3},{1,0},{2,1},{3,2},{4,7},{5,4},{6,5},{7,6},{8,11},{9,8},{10,9... | collective-permute-start | bytes 995336 | tf_op jit(solution)/shard_map/ppermute | solution.py:849
  (55 other events, 564.7 us)
Sparse Core Ops, SparseCore 0:
  10.1 39.2 all-gather.4
  51.9 61.2 all-gather.6
  115.1 27.7 all-gather.8
  167.1 57.3 reduce-scatter.2
  251.0 58.7 reduce-scatter.4
where the time goes:
time: 335 us; the launch traced here: 333 us
  Pallas kernels  124 us (37%)
  starting transfers between devices  88.5 us (26%)
  waiting for transfers between devices  72.9 us (22%)
  local copies, waits for them, and re-layouts  15 us (4%)
  between operations  14.5 us (4%)
  blocking collectives  10.1 us (3%)
  other arithmetic  6.96 us (2%)
    pallas_call x22, Pallas kernels, call(): pl.pallas_call(kernel, out_shape=tuple((pltpu.HBM(o.shape, o.dtype) for o...  124 us
    ppermute x15, starting transfers between devices, tp_scatter(): lax.ppermute(chunks[r], 'tp', [(i, (i - r) % tp) for i in range(tp)])  36.4 us
    ppermute x18, starting transfers between devices, tp_gather(): lax.ppermute(value, 'tp', [(i, (i + k) % tp) for i in range(tp)])  33.7 us
    ppermute x15, waiting for transfers between devices, tp_scatter(): lax.ppermute(chunks[r], 'tp', [(i, (i - r) % tp) for i in range(tp)])  29.5 us
    ppermute x18, waiting for transfers between devices, tp_gather(): lax.ppermute(value, 'tp', [(i, (i + k) % tp) for i in range(tp)])  26.5 us
    ppermute x17, starting transfers between devices, seq_xor(): return lax.ppermute(value, 'seq', [(i, i ^ mask) for i in range(nseq)])  18.2 us
    ppermute x17, waiting for transfers between devices, seq_xor(): return lax.ppermute(value, 'seq', [(i, i ^ mask) for i in range(nseq)])  16.7 us
    all_gather x1, blocking collectives, shards(): blocks = lax.all_gather(block, 'seq', axis=0)  10.1 us
  transfers between devices with their start and end apart: 55, of which 24 were waited for; matrix products, arithmetic and copies ran while one was open for 6% of the time, Pallas kernels for 36%

commit v1 on v0

--- a/solution.py
+++ b/solution.py
@@ -500,7 +500,7 @@
 
 def mlp_both(tp, inner, scalars, ins, outs):
     pieces = ins[:tp]
-    first, low_first, g3, hot, mods, w_out2, w_up, w_down, turned = ins[tp:]
+    hot, mods, g3, w_out2, first, low_first, w_up, w_down, turned = ins[tp:]
     x2_o, mlp_o, hid_o, db3_o, dpre_o, sums_o = outs[:6]
     dm_o, b3_o = outs[6 : 6 + tp], outs[6 + tp :]
     own, width = x2_o.shape
@@ -616,7 +616,7 @@
 def frame_back(tp, inner, scalars, ins, outs):
     pieces = ins[:tp]
     (rank,) = scalars
-    d_b2, g2, hot, mods, w_q2, w_far, w_a, qkv, prob, tok, own_b1, sums, gate2, turned = ins[tp:]
+    w_q2, w_far, hot, mods, d_b2, g2, w_a, qkv, prob, tok, own_b1, sums, gate2, turned = ins[tp:]
     g1_o, db1_o, dqkv_o = outs[:3]
     da_o = outs[3:-6]
     heads, grads, made, cqs, norms, found = outs[-6:]
@@ -797,7 +797,7 @@
 def place_captions(clips, scalars, ins, outs):
     (cap_len,) = scalars
     parts, condition = ins
-    out_o, cond_o, rows = outs
+    out_o, cond_o, rows, turned = outs
     slots = out_o.shape[2]
     keys, feats = rows.shape
     blocks = parts.shape[0]
@@ -816,10 +816,11 @@
     slot = lax.broadcasted_iota(jnp.int32, (keys, slots), 1)
     key = lax.broadcasted_iota(jnp.int32, (keys, slots), 0)
     target = out_o.bufs[0]
+    turned[...] = rows[...].T
 
     def some(c, start):
         pick = (slot + start == key) & (slot < cap_len[c])
-        target[c] = dot_tn(rows[...], jnp.where(pick, 1.0, 0.0).astype(BF16))
+        target[c] = dot_nn(turned[...], jnp.where(pick, 1.0, 0.0).astype(BF16))
         return start + cap_len[c]
 
     lax.fori_loop(0, clips, some, jnp.int32(0))
@@ -964,7 +965,7 @@
         for g in range(groups)
     ]
     z_rest = tp_gather(jnp.concatenate([z_pack] + mod_rows, axis=0), tp)
-    z_rest = lax.optimization_barrier((*z_rest, tok, cap, *far_a[1:]))[:tp]
+    z_rest = lax.optimization_barrier((*z_rest, tok, *far_a[1:]))[:tp]
     (mods,) = call(
         part(modulations, tp, clips, drows),
         [sds((6, clip_pad, width), F32)],
@@ -1005,6 +1006,7 @@
         part(first_rows, tp),
         [sds((own, width), F32), sds((own, width)), sds((own, width), F32)],
         [*far(branch_parts), tok, hot, mods],
+        order=[cap],
         name="first_rows",
     )
     low_parts = tp_gather(low_own, tp)
@@ -1045,12 +1047,12 @@
         + [sds((own, width))] * (2 * tp),
         [
             *far(cross_parts),
+            hot,
+            mods,
+            g3,
+            Cols(full_c, 0, width),
             x1_own,
             first_low,
-            g3,
-            hot,
-            mods,
-            Cols(full_c, 0, width),
             Cols(full_c, width, lane(hid)),
             Cols(full_c, width + lane(hid), lane(hid)),
             turned,
@@ -1109,22 +1111,18 @@
     half = nseq // 2
     kv_away = seq_xor(kv_rel[half:], 1, nseq)
     kv_sums = (kv_rel[:half].astype(F32) + kv_away.astype(F32)).astype(BF16)
-    kv_own = kv_sums[0].astype(F32)
-    for c in range(1, half):
-        kv_own = kv_own + seq_xor(kv_sums[c], 2 * c, nseq).astype(F32)
-    kv_own = kv_own.astype(BF16)
     outs = call(
         part(frame_back, tp, inner),
         [sds((own, width), F32), sds((rows, width)), sds((rows, 3 * inner))]
         + [sds((own + clip_pad * -(-mod_size // width), width))] * tp,
         [
             *far(dcq_parts),
+            w_q2,
+            w_d,
+            hot,
+            mods,
             d_b2,
             g2_own,
-            hot,
-            mods,
-            w_q2,
-            w_d,
             w_a,
             qkv,
             probs,
@@ -1167,6 +1165,19 @@
         [sum_one],
         name="finish_mlp",
     )
+    both_own, mod_cols = call(
+        part(token_rows, tp),
+        [sds((2 * own, width)), sds((clip_pad, mod_size), F32)],
+        [*far(da_parts), *far(b3_parts), tok, g1_own, hot, mods, x2_own, live],
+        order=[grad_three],
+        name="token_rows",
+    )
+    both_parts = tp_gather(both_own, tp)
+    kv_sums = after(kv_sums, both_own)
+    kv_own = kv_sums[0].astype(F32)
+    for c in range(1, half):
+        kv_own = kv_own + seq_xor(kv_sums[c], 2 * c, nseq).astype(F32)
+    kv_own = kv_own.astype(BF16)
     feats = width // tp
     cap_chunks = call(
         part(caption_chunks, tp),
@@ -1175,14 +1186,6 @@
         smem=[rank],
         name="caption_chunks",
     )
-    both_own, mod_cols = call(
-        part(token_rows, tp),
-        [sds((2 * own, width)), sds((clip_pad, mod_size), F32)],
-        [*far(da_parts), *far(b3_parts), tok, g1_own, hot, mods, x2_own, live],
-        order=[grad_three, grad_up, cap_chunks[0]],
-        name="token_rows",
-    )
-    both_parts = tp_gather(both_own, tp)
     mod_cols = seq_total(mod_cols, nseq)
 
     span = max(feats, 2 * drows)
@@ -1190,6 +1193,7 @@
         ada_grads,
         [sds(w_ada.shape, F32), sds((clip_pad, span))],
         [Near(mod_cols), Near(padded(scaled_own, clip_pad, 0)), w_ada],
+        order=[grad_up],
         name="ada_grads",
     )
     shared = [jnp.concatenate([padded(c, span, 1), cond_rows], axis=0) for c in cap_chunks]
@@ -1214,7 +1218,7 @@
         part(place_captions, clips),
         [sds((clips, feats, slots), F32), sds((clips, width), F32)],
         [Near(blocks), condition],
-        work=[sds((keys, feats))],
+        work=[sds((keys, feats)), sds((feats, keys))],
         smem=[cap_len],
         order=[output, grad_ada],
         name="place_captions",

time: 335 us -> 321 us (0.958)
  starting transfers between devices: 88.5 us -> 75 us
    ppermute x18, waiting for transfers between devices: 26.5 us -> 39.3 us  [tp_gather(): lax.ppermute(value, 'tp', [(i, (i + k) % tp) for i in range(tp)])]
    ppermute x15, waiting for transfers between devices: 29.5 us -> 21.5 us  [tp_scatter(): lax.ppermute(chunks[r], 'tp', [(i, (i - r) % tp) for i in range(tp)])]
    ppermute x15, starting transfers between devices: 36.4 us -> 29.1 us  [tp_scatter(): lax.ppermute(chunks[r], 'tp', [(i, (i - r) % tp) for i in range(tp)])]
    ppermute x18, starting transfers between devices: 33.7 us -> 29.7 us  [tp_gather(): lax.ppermute(value, 'tp', [(i, (i + k) % tp) for i in range(tp)])]
    unnamed x51 -> x45, local copies, waits for them, and re-layouts: 8.94 us -> 7.09 us
  transfers between devices with their start and end apart: 55 -> 55, of which waited for: 24 -> 22; matrix products, arithmetic and copies ran while one was open for 6% -> 5% of each run, Pallas kernels for 36% -> 38%
where the time goes in v1:
time: 321 us; the launch traced here: 320 us
  Pallas kernels  124 us (39%)
  starting transfers between devices  75 us (23%)
  waiting for transfers between devices  74.7 us (23%)
  between operations  14.4 us (4%)
  local copies, waits for them, and re-layouts  13.2 us (4%)
  blocking collectives  10.2 us (3%)
  other arithmetic  7.17 us (2%)
    pallas_call x22, Pallas kernels, call(): pl.pallas_call(kernel, out_shape=tuple((pltpu.HBM(o.shape, o.dtype) for o...  124 us
    ppermute x18, waiting for transfers between devices, tp_gather(): lax.ppermute(value, 'tp', [(i, (i + k) % tp) for i in range(tp)])  39.3 us
    ppermute x18, starting transfers between devices, tp_gather(): lax.ppermute(value, 'tp', [(i, (i + k) % tp) for i in range(tp)])  29.7 us
    ppermute x15, starting transfers between devices, tp_scatter(): lax.ppermute(chunks[r], 'tp', [(i, (i - r) % tp) for i in range(tp)])  29.1 us
    ppermute x15, waiting for transfers between devices, tp_scatter(): lax.ppermute(chunks[r], 'tp', [(i, (i - r) % tp) for i in range(tp)])  21.5 us
    ppermute x17, starting transfers between devices, seq_xor(): return lax.ppermute(value, 'seq', [(i, i ^ mask) for i in range(nseq)])  16 us
    ppermute x17, waiting for transfers between devices, seq_xor(): return lax.ppermute(value, 'seq', [(i, i ^ mask) for i in range(nseq)])  13.8 us
    all_gather x1, blocking collectives, shards(): blocks = lax.all_gather(block, 'seq', axis=0)  10.2 us
  transfers between devices with their start and end apart: 55, of which 22 were waited for; matrix products, arithmetic and copies ran while one was open for 5% of the time, Pallas kernels for 38%

profile of v1, /device:TPU:0, one launch (start us, length us, event | category | flops | bytes accessed | tf_op | source)
XLA Modules:
  0.0 319.5 jit_solution(4856070582229500666)
XLA Ops:
  41.1 6.6 %collective-permute-done.8.refs_12_.refs_17_ = bf16[144,1152]{1,0:T(8,128)(2,1)S(1)} collective-permute-done((bf16[144,1152]{1,0:T(8,128)(2,1)S(1)}, bf16[144,1152]{1,0:T(8,128)(2,1)S(1)}, u32[]{:S(2)}, u32[]{:S(2)}) %collective-permute-start.8) | collective-permute-done | bytes 331808 | tf_op jit(solution)/shard_map/ppermute | solution.py:861
  55.9 8.9 %frame_forward.1 = (bf16[288,1152]{1,0:T(8,128)(2,1)}, bf16[288,864]{1,0:T(8,128)(2,1)}, bf16[4,288,288]{2,1,0:T(8,128)(2,1)}, bf16[288,288]{1,0:T(8,128)(2,1)},...) custom-call(s32[2]{0:T(128)S(1)} %pad_add_fusion.refs_0_, ...), custom_call_target="tpu_custom_call" | custom-call | bytes 6200064 | tf_op jit(solution)/shard_map/frame_forward/pallas_call | solution.py:180
  71.2 7.6 %live_captions.1 = (bf16[640,1152]{1,0:T(8,128)(2,1)}, s32[1,640]{1,0:T(1,128)}) custom-call(s32[4]{0:T(128)S(1)} %copy-done, bf16[4,300,1152]{2,1,0:T(8,128)(2,1)} %copy.31.refs_1_), custom_call_target="tpu_custom_call" | custom-call | bytes 4241920 | tf_op jit(solution)/shard_map/live_captions/pallas_call | solution.py:180
  91.2 5.0 %key_values.1.refs_7_ = bf16[640,576]{1,0:T(8,128)(2,1)} custom-call(bf16[640,1152]{1,0:T(8,128)(2,1)} %get-tuple-element.119.refs_7_.refs_0_.refs_2_, bf16[1152,960]{1,0:T(8,128)(2,1)} %all-gather.5.cloned.1.call-done.refs_1_.refs_6_.refs_5_), custom_call_target="tpu_custom_call" | custom-call | bytes 4423680 | tf_op jit(solution)/shard_map/key_values/pallas_call | solution.py:180
  96.1 4.4 %collective-permute-done.17.refs_2_ = bf16[72,1152]{1,0:T(8,128)(2,1)S(1)} collective-permute-done((bf16[72,1152]{1,0:T(8,128)(2,1)}, bf16[72,1152]{1,0:T(8,128)(2,1)S(1)}, u32[]{:S(2)}, u32[]{:S(2)}) %collective-permute-start.17) | collective-permute-done | bytes 165920 | tf_op jit(solution)/shard_map/ppermute | solution.py:850
  100.6 7.6 %cross_forward.1 = (bf16[288,1152]{1,0:T(8,128)(2,1)}, bf16[288,288]{1,0:T(8,128)(2,1)}, bf16[4,288,640]{2,1,0:T(8,128)(2,1)}, bf16[288,288]{1,0:T(8,128)(2,1)}, bf16[72,1152]{1,0:T(8,128)(2,1)}) custom-call(bf16[72,1152]{1,0:T(8,128)(2,1)} %get-tuple-element.120.refs_0_, bf16[72,1152]{1,0:T(8,128)(2,1)S(1)} %collective-permute-done.16.refs_1_, ...), custom_call_target="tpu_custom_call" | custom-call | bytes 6252160 | tf_op jit(solution)/shard_map/cross_forward/pallas_call | solution.py:180
  114.2 4.7 %collective-permute-done.19.refs_2_ = bf16[72,1152]{1,0:T(8,128)(2,1)S(1)} collective-permute-done((bf16[72,1152]{1,0:T(8,128)(2,1)}, bf16[72,1152]{1,0:T(8,128)(2,1)S(1)}, u32[]{:S(2)}, u32[]{:S(2)}) %collective-permute-start.19) | collective-permute-done | bytes 165920 | tf_op jit(solution)/shard_map/ppermute | solution.py:850
  118.9 5.1 %collective-permute-done.20.refs_3_ = bf16[72,1152]{1,0:T(8,128)(2,1)S(1)} collective-permute-done((bf16[72,1152]{1,0:T(8,128)(2,1)}, bf16[72,1152]{1,0:T(8,128)(2,1)S(1)}, u32[]{:S(2)}, u32[]{:S(2)}) %collective-permute-start.20) | collective-permute-done | bytes 165920 | tf_op jit(solution)/shard_map/ppermute | solution.py:850
  124.0 12.6 %mlp_both.1 = (f32[72,1152]{1,0:T(8,128)}, bf16[288,1152]{1,0:T(8,128)(2,1)}, bf16[288,1152]{1,0:T(8,128)(2,1)}, bf16[288,1152]{1,0:T(8,128)(2,1)}, bf16[288,115...) custom-call(s32[2]{0:T(128)S(1)} %pad_add_fusion.refs_0_, ...), custom_call_target="tpu_custom_call" | custom-call | bytes 30790656 | tf_op jit(solution)/shard_map/mlp_both/pallas_call | solution.py:180
  136.7 5.1 %collective-permute-start.22 = (bf16[72,1152]{1,0:T(8,128)(2,1)}, bf16[72,1152]{1,0:T(8,128)(2,1)S(1)}, u32[]{:S(2)}, u32[]{:S(2)}) collective-permute-start(bf16[72,1152]{1,0:T(8,128)(2,1)} %get-tuple-element.129), channel_id=1, source_target_pairs={{0,3},{1,0},{2,1},{3,2},{4,7},{5,4},{6,5},{7,6},{8,11},{9,8},{10,9... | collective-permute-start | bytes 497672 | tf_op jit(solution)/shard_map/ppermute | solution.py:856
  142.5 9.0 %grads_mlp.1.refs_9_ = bf16[1152,2304]{1,0:T(8,128)(2,1)} custom-call(bf16[288,1152]{1,0:T(8,128)(2,1)} %get-tuple-element.133.refs_0_, bf16[288,1152]{1,0:T(8,128)(2,1)} %get-tuple-element.134.refs_1_, bf16[288,1152]{1,0:T(8,128)(2,1)} %get-tuple-element.135.refs_2_, bf16[288,1152]{1,0:T(8,128)(2,1)} %get-tuple-element.136.refs_3_), custom_call_target="tpu_custom_call" | custom-call | bytes 7962624 | tf_op jit(solution)/shard_map/grads_mlp/pallas_call | solution.py:180
  151.5 5.8 %collective-permute-done.23.refs_2_ = bf16[72,1152]{1,0:T(8,128)(2,1)S(1)} collective-permute-done((bf16[72,1152]{1,0:T(8,128)(2,1)}, bf16[72,1152]{1,0:T(8,128)(2,1)S(1)}, u32[]{:S(2)}, u32[]{:S(2)}) %collective-permute-start.23) | collective-permute-done | bytes 165920 | tf_op jit(solution)/shard_map/ppermute | solution.py:856
  164.8 5.2 %collective-permute-done.25.refs_2_ = bf16[72,1152]{1,0:T(8,128)(2,1)S(1)} collective-permute-done((bf16[72,1152]{1,0:T(8,128)(2,1)S(1)}, bf16[72,1152]{1,0:T(8,128)(2,1)S(1)}, u32[]{:S(2)}, u32[]{:S(2)}) %collective-permute-start.25) | collective-permute-done | bytes 165920 | tf_op jit(solution)/shard_map/ppermute | solution.py:850
  170.1 5.4 %collective-permute-done.26.refs_3_ = bf16[72,1152]{1,0:T(8,128)(2,1)S(1)} collective-permute-done((bf16[72,1152]{1,0:T(8,128)(2,1)S(1)}, bf16[72,1152]{1,0:T(8,128)(2,1)S(1)}, u32[]{:S(2)}, u32[]{:S(2)}) %collective-permute-start.26) | collective-permute-done | bytes 165920 | tf_op jit(solution)/shard_map/ppermute | solution.py:850
  175.5 10.1 %cross_back.1 = (bf16[288,1152]{1,0:T(8,128)(2,1)}, bf16[288,288]{1,0:T(8,128)(2,1)}, bf16[640,576]{1,0:T(8,128)(2,1)}, bf16[72,1152]{1,0:T(8,128)(2,1)}, bf16[8,80,576]{2,1,0:T(8,128)(2,1)}) custom-call(s32[2]{0:T(128)S(1)} %pad_add_fusion.refs_0_, bf16[72,1152]{1,0:T(8,128)(2,1)} %get-tuple-element.137.refs_1_, ...), custom_call_target="tpu_custom_call" | custom-call | bytes 13473792 | tf_op jit(solution)/shard_map/cross_back/pallas_call | solution.py:180
  192.3 9.0 %grads_cross.1 = bf16[1152,2304]{1,0:T(8,128)(2,1)} custom-call(bf16[288,1152]{1,0:T(8,128)(2,1)} %get-tuple-element.126.refs_10_.refs_0_, bf16[288,288]{1,0:T(8,128)(2,1)} %get-tuple-element.151.refs_1_, bf16[640,1152]{1,0:T(8,128)(2,1)} %get-tuple-element.119.refs_7_.refs_0_.refs_2_, bf16[640,576]{1,0:T(8,128)(2,1)} %get-tuple-element.152.refs_3_, ...), custom_call_target="tpu_custom_call" | custom-call | bytes 9179136 | tf_op jit(solution)/shard_map/grads_cross/pallas_call | solution.py:180
  202.6 5.3 %collective-permute-start.32 = (bf16[72,1152]{1,0:T(8,128)(2,1)S(1)}, bf16[72,1152]{1,0:T(8,128)(2,1)S(1)}, u32[]{:S(2)}, u32[]{:S(2)}) collective-permute-start(bf16[72,1152]{1,0:T(8,128)(2,1)S(1)} %copy-done.18), channel_id=1, source_target_pairs={{0,3},{1,0},{2,1},{3,2},{4,7},{5,4},{6,5},{7,6},{8,11},{9,8},{10,9... | collective-permute-start | bytes 497672 | tf_op jit(solution)/shard_map/ppermute | solution.py:856
  208.7 13.7 %frame_back.1 = (f32[72,1152]{1,0:T(8,128)}, bf16[288,1152]{1,0:T(8,128)(2,1)}, bf16[288,864]{1,0:T(8,128)(2,1)}, bf16[88,1152]{1,0:T(8,128)(2,1)}, bf16[88,1152...) custom-call(s32[2]{0:T(128)S(1)} %pad_add_fusion.refs_0_, ...), custom_call_target="tpu_custom_call" | custom-call | bytes 13317120 | tf_op jit(solution)/shard_map/frame_back/pallas_call | solution.py:180
  229.2 7.3 %grads_frame.1.refs_14_ = bf16[1152,2304]{1,0:T(8,128)(2,1)} custom-call(bf16[288,1152]{1,0:T(8,128)(2,1)} %get-tuple-element.170.refs_0_, bf16[288,864]{1,0:T(8,128)(2,1)} %get-tuple-element.171.refs_1_, bf16[288,1152]{1,0:T(8,128)(2,1)} %get-tuple-element.172.refs_2_, bf16[288,288]{1,0:T(8,128)(2,1)} %get-tuple-element.173.refs_3_, ...), custom_call_target="tpu_custom_call", output_to_operand_aliasing={{}: (4, {})} | custom-call | bytes 7299072 | tf_op jit(solution)/shard_map/grads_frame/pallas_call | solution.py:180
  236.5 7.5 %collective-permute-done.36.refs_2_ = bf16[88,1152]{1,0:T(8,128)(2,1)S(1)} collective-permute-done((bf16[88,1152]{1,0:T(8,128)(2,1)}, bf16[88,1152]{1,0:T(8,128)(2,1)S(1)}, u32[]{:S(2)}, u32[]{:S(2)}) %collective-permute-start.36) | collective-permute-done | bytes 202784 | tf_op jit(solution)/shard_map/ppermute | solution.py:856
  270.0 8.6 %collective-permute-done.39.refs_3_ = bf16[144,1152]{1,0:T(8,128)(2,1)S(1)} collective-permute-done((bf16[144,1152]{1,0:T(8,128)(2,1)}, bf16[144,1152]{1,0:T(8,128)(2,1)S(1)}, u32[]{:S(2)}, u32[]{:S(2)}) %collective-permute-start.39) | collective-permute-done | bytes 331808 | tf_op jit(solution)/shard_map/ppermute | solution.py:850
  278.6 7.7 %collective-permute-start.47 = (bf16[88,288]{1,0:T(8,128)(2,1)S(1)}, bf16[88,288]{1,0:T(8,128)(2,1)S(1)}, u32[]{:S(2)}, u32[]{:S(2)}) collective-permute-start(bf16[88,288]{1,0:T(8,128)(2,1)S(1)} %get-tuple-element.185), channel_id=1, source_target_pairs={{0,3},{1,0},{2,1},{3,2},{4,7},{5,4},{6,5},{7,6},{8,11},{9,8},{10,9... | collective-permute-start | bytes 152072 | tf_op jit(solution)/shard_map/ppermute | solution.py:856
  295.7 10.2 %all-gather = bf16[704,288]{1,0:T(8,128)(2,1)S(1)} all-gather(bf16[88,288]{1,0:T(8,128)(2,1)} %join_rows.1), channel_id=2, replica_groups=mesh['seq'=8,'tp'=4] {'seq'}, dimensions={0}, use_global_device_ids=true | all-gather | bytes 456192 | tf_op jit(solution)/shard_map/all_gather | solution.py:1207
  305.8 4.3 %place_captions.1 = (f32[4,288,300]{2,1,0:T(8,128)}, f32[4,1152]{1,0:T(4,128)}) custom-call(s32[4]{0:T(128)S(1)} %copy-done, bf16[8,88,288]{2,1,0:T(8,128)(2,1)S(1)} %bitcast.26, f32[4,1152]{1,0:T(4,128)} %refs_2_.5, bf16[17,16,1152]{2,1,0:T(8,128)(2,1)} %get-tuple-element.175.refs_3_, f32[144,1728]{1,0:T(8,128)} %get-tuple-element.105.refs_4_), custom_call_target="tpu_custom_call" | custom-call | bytes 1824768 | tf_op jit(solution)/shard_map/place_captions/pallas_call | solution.py:180
  (189 shorter events, 128.4 us)
Async XLA Ops:
  7.2 84.0 %all-gather.5.cloned.1.call-start = ((), (), s32[]{:S(2)}) async-start(), calls=%async_computation.2 | async-start | bytes 2654208 | tf_op jit(solution)/shard_map/all_gather | solution.py:952
  10.1 114.0 %all-gather.7.cloned.1.call-start = ((), (), s32[]{:S(2)}) async-start(), calls=%async_computation.3 | async-start | bytes 8957952 | tf_op jit(solution)/shard_map/all_gather | solution.py:981
  25.0 15.9 %collective-permute-start.6 = (bf16[144,1152]{1,0:T(8,128)(2,1)S(1)}, bf16[144,1152]{1,0:T(8,128)(2,1)S(1)}, u32[]{:S(2)}, u32[]{:S(2)}) collective-permute-start(bf16[144,1152]{1,0:T(8,128)(2,1)S(1)} %pad_maximum_fusion.refs_6_.refs_11_), channel_id=1, source_target_pairs={{0,8},{4,12},{8,0},{12,4},{16,24},{20,28},{24,16},{28,20},{1,9},{5... | collective-permute-start | bytes 995336 | tf_op jit(solution)/shard_map/ppermute | solution.py:861
  26.6 14.6 %collective-permute-start.7 = (bf16[144,1152]{1,0:T(8,128)(2,1)S(1)}, bf16[144,1152]{1,0:T(8,128)(2,1)S(1)}, u32[]{:S(2)}, u32[]{:S(2)}) collective-permute-start(bf16[144,1152]{1,0:T(8,128)(2,1)S(1)} %pad_maximum_fusion.refs_6_.refs_11_), channel_id=1, source_target_pairs={{0,16},{4,20},{8,24},{12,28},{16,0},{20,4},{24,8},{28,12},{1,17},{... | collective-permute-start | bytes 995336 | tf_op jit(solution)/shard_map/ppermute | solution.py:861
  28.3 19.4 %collective-permute-start.8 = (bf16[144,1152]{1,0:T(8,128)(2,1)S(1)}, bf16[144,1152]{1,0:T(8,128)(2,1)S(1)}, u32[]{:S(2)}, u32[]{:S(2)}) collective-permute-start(bf16[144,1152]{1,0:T(8,128)(2,1)S(1)} %pad_maximum_fusion.refs_6_.refs_11_), channel_id=1, source_target_pairs={{0,24},{4,28},{8,16},{12,20},{16,8},{20,12},{24,0},{28,4},{1,25},{... | collective-permute-start | bytes 995336 | tf_op jit(solution)/shard_map/ppermute | solution.py:861
  51.1 157.6 %all-gather.9.cloned.1.call-start = ((), (), s32[]{:S(2)}) async-start(), calls=%async_computation.4 | async-start | bytes 2322432 | tf_op jit(solution)/shard_map/all_gather | solution.py:982
  52.0 211.5 %reduce-scatter.3.cloned.1.call-start = ((), (), s32[]{:S(2)}) async-start(), calls=%async_computation.5 | async-start | bytes 5971968 | tf_op jit(solution)/shard_map/reduce_scatter | solution.py:1081
  68.2 14.8 %collective-permute-start.14 = (bf16[72,1152]{1,0:T(8,128)(2,1)}, bf16[72,1152]{1,0:T(8,128)(2,1)S(1)}, u32[]{:S(2)}, u32[]{:S(2)}) collective-permute-start(bf16[72,1152]{1,0:T(8,128)(2,1)} %get-tuple-element.117), channel_id=1, source_target_pairs={{0,2},{1,3},{2,0},{3,1},{4,6},{5,7},{6,4},{7,5},{8,10},{9,11},{10,... | collective-permute-start | bytes 497672 | tf_op jit(solution)/shard_map/ppermute | solution.py:856
  68.2 14.8 %collective-permute-start.15 = (bf16[72,1152]{1,0:T(8,128)(2,1)}, bf16[72,1152]{1,0:T(8,128)(2,1)S(1)}, u32[]{:S(2)}, u32[]{:S(2)}) collective-permute-start(bf16[72,1152]{1,0:T(8,128)(2,1)} %get-tuple-element.118), channel_id=1, source_target_pairs={{0,1},{1,2},{2,3},{3,0},{4,5},{5,6},{6,7},{7,4},{8,9},{9,10},{10,1... | collective-permute-start | bytes 497672 | tf_op jit(solution)/shard_map/ppermute | solution.py:856
  136.7 14.8 %collective-permute-start.22 = (bf16[72,1152]{1,0:T(8,128)(2,1)}, bf16[72,1152]{1,0:T(8,128)(2,1)S(1)}, u32[]{:S(2)}, u32[]{:S(2)}) collective-permute-start(bf16[72,1152]{1,0:T(8,128)(2,1)} %get-tuple-element.129), channel_id=1, source_target_pairs={{0,3},{1,0},{2,1},{3,2},{4,7},{5,4},{6,5},{7,6},{8,11},{9,8},{10,9... | collective-permute-start | bytes 497672 | tf_op jit(solution)/shard_map/ppermute | solution.py:856
  141.8 15.4 %collective-permute-start.23 = (bf16[72,1152]{1,0:T(8,128)(2,1)}, bf16[72,1152]{1,0:T(8,128)(2,1)S(1)}, u32[]{:S(2)}, u32[]{:S(2)}) collective-permute-start(bf16[72,1152]{1,0:T(8,128)(2,1)} %get-tuple-element.130), channel_id=1, source_target_pairs={{0,2},{1,3},{2,0},{3,1},{4,6},{5,7},{6,4},{7,5},{8,10},{9,11},{10,... | collective-permute-start | bytes 497672 | tf_op jit(solution)/shard_map/ppermute | solution.py:856
  142.2 15.0 %collective-permute-start.24 = (bf16[72,1152]{1,0:T(8,128)(2,1)}, bf16[72,1152]{1,0:T(8,128)(2,1)S(1)}, u32[]{:S(2)}, u32[]{:S(2)}) collective-permute-start(bf16[72,1152]{1,0:T(8,128)(2,1)} %get-tuple-element.131), channel_id=1, source_target_pairs={{0,1},{1,2},{2,3},{3,0},{4,5},{5,6},{6,7},{7,4},{8,9},{9,10},{10,1... | collective-permute-start | bytes 497672 | tf_op jit(solution)/shard_map/ppermute | solution.py:856
  160.1 150.0 %reduce-scatter.5.cloned.1.call-start = ((), (), s32[]{:S(2)}) async-start(), calls=%async_computation.6 | async-start | bytes 5971968 | tf_op jit(solution)/shard_map/reduce_scatter | solution.py:1159
  161.0 14.4 %collective-permute-start.26 = (bf16[72,1152]{1,0:T(8,128)(2,1)S(1)}, bf16[72,1152]{1,0:T(8,128)(2,1)S(1)}, u32[]{:S(2)}, u32[]{:S(2)}) collective-permute-start(bf16[72,1152]{1,0:T(8,128)(2,1)S(1)} %copy-done.14), channel_id=1, source_target_pairs={{0,2},{1,3},{2,0},{3,1},{4,6},{5,7},{6,4},{7,5},{8,10},{9,11},{10,... | collective-permute-start | bytes 497672 | tf_op jit(solution)/shard_map/ppermute | solution.py:850
  186.6 21.9 %collective-permute-start.31 = (bf16[4,80,576]{2,1,0:T(8,128)(2,1)S(1)}, bf16[4,80,576]{2,1,0:T(8,128)(2,1)S(1)}, u32[]{:S(2)}, u32[]{:S(2)}) collective-permute-start(bf16[4,80,576]{2,1,0:T(8,128)(2,1)S(1)} %slice.77), channel_id=1, source_target_pairs={{0,4},{4,0},{8,12},{12,8},{16,20},{20,16},{24,28},{28,24},{1,5},{5... | collective-permute-start | bytes 1105928 | tf_op jit(solution)/shard_map/ppermute | solution.py:861
  186.7 14.6 %collective-permute-start.28 = (bf16[72,1152]{1,0:T(8,128)(2,1)}, bf16[72,1152]{1,0:T(8,128)(2,1)S(1)}, u32[]{:S(2)}, u32[]{:S(2)}) collective-permute-start(bf16[72,1152]{1,0:T(8,128)(2,1)} %get-tuple-element.140.refs_1_), channel_id=1, source_target_pairs={{0,1},{1,2},{2,3},{3,0},{4,5},{5,6},{6,7},{7,4},{8,9},{9,10},{10,1... | collective-permute-start | bytes 497672 | tf_op jit(solution)/shard_map/ppermute | solution.py:850
  202.6 19.8 %collective-permute-start.32 = (bf16[72,1152]{1,0:T(8,128)(2,1)S(1)}, bf16[72,1152]{1,0:T(8,128)(2,1)S(1)}, u32[]{:S(2)}, u32[]{:S(2)}) collective-permute-start(bf16[72,1152]{1,0:T(8,128)(2,1)S(1)} %copy-done.18), channel_id=1, source_target_pairs={{0,3},{1,0},{2,1},{3,2},{4,7},{5,4},{6,5},{7,6},{8,11},{9,8},{10,9... | collective-permute-start | bytes 497672 | tf_op jit(solution)/shard_map/ppermute | solution.py:856
  207.9 15.0 %collective-permute-start.33 = (bf16[72,1152]{1,0:T(8,128)(2,1)S(1)}, bf16[72,1152]{1,0:T(8,128)(2,1)S(1)}, u32[]{:S(2)}, u32[]{:S(2)}) collective-permute-start(bf16[72,1152]{1,0:T(8,128)(2,1)S(1)} %copy-done.17), channel_id=1, source_target_pairs={{0,2},{1,3},{2,0},{3,1},{4,6},{5,7},{6,4},{7,5},{8,10},{9,11},{10,... | collective-permute-start | bytes 497672 | tf_op jit(solution)/shard_map/ppermute | solution.py:856
  208.1 14.8 %collective-permute-start.34 = (bf16[72,1152]{1,0:T(8,128)(2,1)S(1)}, bf16[72,1152]{1,0:T(8,128)(2,1)S(1)}, u32[]{:S(2)}, u32[]{:S(2)}) collective-permute-start(bf16[72,1152]{1,0:T(8,128)(2,1)S(1)} %copy-done.16), channel_id=1, source_target_pairs={{0,1},{1,2},{2,3},{3,0},{4,5},{5,6},{6,7},{7,4},{8,9},{9,10},{10,1... | collective-permute-start | bytes 497672 | tf_op jit(solution)/shard_map/ppermute | solution.py:856
  225.9 18.1 %collective-permute-start.36 = (bf16[88,1152]{1,0:T(8,128)(2,1)}, bf16[88,1152]{1,0:T(8,128)(2,1)S(1)}, u32[]{:S(2)}, u32[]{:S(2)}) collective-permute-start(bf16[88,1152]{1,0:T(8,128)(2,1)} %get-tuple-element.163), channel_id=1, source_target_pairs={{0,2},{1,3},{2,0},{3,1},{4,6},{5,7},{6,4},{7,5},{8,10},{9,11},{10,... | collective-permute-start | bytes 608264 | tf_op jit(solution)/shard_map/ppermute | solution.py:856
  226.8 17.2 %collective-permute-start.37 = (bf16[88,1152]{1,0:T(8,128)(2,1)}, bf16[88,1152]{1,0:T(8,128)(2,1)S(1)}, u32[]{:S(2)}, u32[]{:S(2)}) collective-permute-start(bf16[88,1152]{1,0:T(8,128)(2,1)} %get-tuple-element.165), channel_id=1, source_target_pairs={{0,1},{1,2},{2,3},{3,0},{4,5},{5,6},{6,7},{7,4},{8,9},{9,10},{10,1... | collective-permute-start | bytes 608264 | tf_op jit(solution)/shard_map/ppermute | solution.py:856
  252.9 17.1 %collective-permute-start.38 = (bf16[144,1152]{1,0:T(8,128)(2,1)}, bf16[144,1152]{1,0:T(8,128)(2,1)S(1)}, u32[]{:S(2)}, u32[]{:S(2)}) collective-permute-start(bf16[144,1152]{1,0:T(8,128)(2,1)} %get-tuple-element.174.refs_1_), channel_id=1, source_target_pairs={{0,1},{1,2},{2,3},{3,0},{4,5},{5,6},{6,7},{7,4},{8,9},{9,10},{10,1... | collective-permute-start | bytes 995336 | tf_op jit(solution)/shard_map/ppermute | solution.py:850
  256.6 22.0 %collective-permute-start.39 = (bf16[144,1152]{1,0:T(8,128)(2,1)}, bf16[144,1152]{1,0:T(8,128)(2,1)S(1)}, u32[]{:S(2)}, u32[]{:S(2)}) collective-permute-start(bf16[144,1152]{1,0:T(8,128)(2,1)} %get-tuple-element.174.refs_1_), channel_id=1, source_target_pairs={{0,2},{1,3},{2,0},{3,1},{4,6},{5,7},{6,4},{7,5},{8,10},{9,11},{10,... | collective-permute-start | bytes 995336 | tf_op jit(solution)/shard_map/ppermute | solution.py:850
  258.5 20.1 %collective-permute-start.40 = (bf16[144,1152]{1,0:T(8,128)(2,1)}, bf16[144,1152]{1,0:T(8,128)(2,1)S(1)}, u32[]{:S(2)}, u32[]{:S(2)}) collective-permute-start(bf16[144,1152]{1,0:T(8,128)(2,1)} %get-tuple-element.174.refs_1_), channel_id=1, source_target_pairs={{0,3},{1,0},{2,1},{3,2},{4,7},{5,4},{6,5},{7,6},{8,11},{9,8},{10,9... | collective-permute-start | bytes 995336 | tf_op jit(solution)/shard_map/ppermute | solution.py:850
  (52 other events, 543.9 us)
Sparse Core Ops, SparseCore 0:
  10.2 39.2 all-gather.4
  52.0 52.0 all-gather.6
  106.0 27.7 all-gather.8
  160.3 55.2 reduce-scatter.2
  244.2 56.2 reduce-scatter.4

commit v2 on v1

--- a/solution.py
+++ b/solution.py
@@ -199,16 +199,13 @@
     return center * inv, inv
 
 
+def high_low(value):
+    high = value.astype(BF16)
+    return jnp.concatenate([high, (value - high.astype(F32)).astype(BF16)], axis=0)
+
+
 def expand(hot, table):
-    high = table.astype(BF16)
-    low = (table - high.astype(F32)).astype(BF16)
-    return dot_nn(hot, high) + dot_nn(hot, low)
-
-
-def split_dot(dot, a, b):
-    high = a.astype(BF16)
-    low = (a - high.astype(F32)).astype(BF16)
-    return dot(high, b) + dot(low, b)
+    return dot_nn(hot, high_low(table))
 
 
 def clip_sums(clips_hot, values):
@@ -320,7 +317,8 @@
         clip_o[at] = clip
         id_o[at] = name
         lane = lax.broadcasted_iota(jnp.int32, (own, hot_o.shape[1]), 1)
-        hot_o[at] = jnp.where(lane == clip, 1.0, 0.0).astype(BF16)
+        pick = (lane == clip) | ((lane == clip + hot_o.shape[1] // 2) & (clip >= 0))
+        hot_o[at] = jnp.where(pick, 1.0, 0.0).astype(BF16)
     key_o[...] = keys
     which = lax.broadcasted_iota(jnp.int32, turned_o.shape, 0)
     turned_o[...] = jnp.where(which == owner, 1.0, 0.0).astype(BF16)
@@ -574,7 +572,7 @@
 def cross_back(tp, inner, scalars, ins, outs):
     (rank,) = scalars
     w_out2, prob, kv, cq = ins[tp:]
-    db2_o, dcq_o, dkv_o, pack_o, rel_o, query, pair, grads, made, scores, back = outs
+    db2_o, dcq_o, dkv_o, pack_o, near_o, away_o, query, pair, grads, made, scores, back, rel = outs
     d_b2 = jnp.concatenate([r[...] for r in ins[:tp]], axis=0)
     db2_o[...] = d_b2
     db2_o.send()
@@ -605,11 +603,14 @@
 
     for_heads(inner // HDIM, two)
     d_kv = jnp.concatenate([take_heads(back.at[0]), take_heads(back.at[1])], axis=1)
-    blocks, size = rel_o.shape[:2]
+    blocks, size = rel.shape[:2]
     for b in range(blocks):
         other = lax.bitwise_xor(rank[1], b)
-        rel_o[(other % 2) * (blocks // 2) + other // 2] = d_kv[b * size : (b + 1) * size]
-    rel_o.send()
+        rel[(other % 2) * (blocks // 2) + other // 2] = d_kv[b * size : (b + 1) * size]
+    away_o[...] = rel[blocks // 2 :]
+    away_o.send()
+    near_o[...] = rel[: blocks // 2]
+    near_o.send()
     dkv_o[...] = d_kv
 
 
@@ -686,15 +687,16 @@
 
 def token_rows(tp, scalars, ins, outs):
     tok, g1, hot, mods, x2, live = ins[2 * tp :]
-    both_o, cols_o = outs
+    tok_o, out_o, cols_o = outs
     own, width = g1.shape
     n, inv = norm_parts(tok[:own].astype(F32))
     scale = 1.0 + expand(hot[:own], mods[1])
     gate = expand(hot[:own], mods[5])
     sums = total(ins[:tp])
-    both_o[:own] = (g1[...] + norm_back(sums[:own] * scale, n, inv)).astype(BF16)
-    both_o[own:] = ((x2[...] + gate * total(ins[tp : 2 * tp])) * live[:own]).astype(BF16)
-    both_o.send()
+    tok_o[...] = (g1[...] + norm_back(sums[:own] * scale, n, inv)).astype(BF16)
+    tok_o.send()
+    out_o[...] = ((x2[...] + gate * total(ins[tp : 2 * tp])) * live[:own]).astype(BF16)
+    out_o.send()
     clips, size = cols_o.shape
     for g in range(-(-size // width)):
         at = own + g * clips
@@ -704,18 +706,15 @@
 
 def place_rows(tp, scalars, ins, outs):
     (rank,) = scalars
-    results, canon = outs[:-1], outs[-1]
-    fmax, seqs = results[0].shape[:2]
+    out, canon = outs
+    fmax, seqs = out.shape[:2]
     own_seqs = seqs // tp
-    own = ins[0].shape[0] // 2
     for k in range(tp):
         canon[lax.rem(rank[0] - k + tp, tp)] = ins[k][...]
-    for i, out in enumerate(results):
-        for f in range(fmax):
-            for q in range(tp):
-                at = i * own + f * own_seqs
-                out[f, q * own_seqs : (q + 1) * own_seqs] = canon[q, at : at + own_seqs]
-        out.send()
+    for f in range(fmax):
+        for q in range(tp):
+            at = f * own_seqs
+            out[f, q * own_seqs : (q + 1) * own_seqs] = canon[q, at : at + own_seqs]
 
 
 def weight_grads(pairs, scalars, ins, outs):
@@ -829,11 +828,12 @@
 def ada_grads(scalars, ins, outs):
     mod_cols, scaled, w_ada = ins
     grad_o, cond_o = outs
-    high = mod_cols[...].astype(BF16)
-    low = (mod_cols[...] - high.astype(F32)).astype(BF16)
-    grad_o[...] = dot_tn(scaled[...], high) + dot_tn(scaled[...], low)
+    both = high_low(mod_cols[...])
+    count = both.shape[0] // 2
+    grad_o[...] = dot_tn(jnp.concatenate([scaled[...], scaled[...]], axis=0), both)
     grad_o.send()
-    cond = split_dot(dot_nt, mod_cols[...], w_ada[...])
+    cond = dot_nt(both, w_ada[...])
+    cond = cond[:count] + cond[count:]
     top = cond.astype(BF16)
     half = cond_o.shape[1] // 2
     cond_o[...] = jnp.zeros(cond_o.shape, BF16)
@@ -926,7 +926,7 @@
         [
             sds((rows, width)),
             sds((rows, width)),
-            sds((rows, clip_pad)),
+            sds((rows, 2 * clip_pad)),
             sds((rows, 1), jnp.int32),
             sds((rows, 1), jnp.int32),
             sds((1, rows), jnp.int32),
@@ -1080,14 +1080,15 @@
     )
     sum_one = lax.psum_scatter(after(grad_one, db2_own), "seq", scatter_dimension=0, tiled=True)
     db2_parts = tp_gather(db2_own, tp)
-    d_b2, d_cq, d_kv, dcq_pack, kv_rel = call(
+    d_b2, d_cq, d_kv, dcq_pack, kv_near, kv_away = call(
         part(cross_back, tp, inner),
         [
             sds((rows, width)),
             sds((rows, inner)),
             sds((keys, 2 * inner)),
             sds((own, tp * inner)),
-            sds((nseq, keys // nseq, 2 * inner)),
+            sds((nseq // 2, keys // nseq, 2 * inner)),
+            sds((nseq // 2, keys // nseq, 2 * inner)),
         ],
         [*far(db2_parts), Cols(full_c, 0, lane(inner)), cprobs, kv, cq],
         work=[
@@ -1097,6 +1098,7 @@
             sds((heads, rows, HDIM)),
             sds((heads, rows, keys)),
             sds((2, heads, keys, HDIM)),
+            sds((nseq, keys // nseq, 2 * inner)),
         ],
         smem=[rank],
         name="cross_back",
@@ -1109,8 +1111,8 @@
         name="grads_cross",
     )
     half = nseq // 2
-    kv_away = seq_xor(kv_rel[half:], 1, nseq)
-    kv_sums = (kv_rel[:half].astype(F32) + kv_away.astype(F32)).astype(BF16)
+    kv_away = seq_xor(kv_away, 1, nseq)
+    kv_sums = (kv_near.astype(F32) + kv_away.astype(F32)).astype(BF16)
     outs = call(
         part(frame_back, tp, inner),
         [sds((own, width), F32), sds((rows, width)), sds((rows, 3 * inner))]
@@ -1165,15 +1167,15 @@
         [sum_one],
         name="finish_mlp",
     )
-    both_own, mod_cols = call(
+    dtok_own, out_own, mod_cols = call(
         part(token_rows, tp),
-        [sds((2 * own, width)), sds((clip_pad, mod_size), F32)],
+        [sds((own, width)), sds((own, width)), sds((clip_pad, mod_size), F32)],
         [*far(da_parts), *far(b3_parts), tok, g1_own, hot, mods, x2_own, live],
         order=[grad_three],
         name="token_rows",
     )
-    both_parts = tp_gather(both_own, tp)
-    kv_sums = after(kv_sums, both_own)
+    dtok_parts = tp_gather(dtok_own, tp)
+    kv_sums = after(kv_sums, dtok_own)
     kv_own = kv_sums[0].astype(F32)
     for c in range(1, half):
         kv_own = kv_own + seq_xor(kv_sums[c], 2 * c, nseq).astype(F32)
@@ -1193,26 +1195,31 @@
         ada_grads,
         [sds(w_ada.shape, F32), sds((clip_pad, span))],
         [Near(mod_cols), Near(padded(scaled_own, clip_pad, 0)), w_ada],
-        order=[grad_up],
         name="ada_grads",
     )
     shared = [jnp.concatenate([padded(c, span, 1), cond_rows], axis=0) for c in cap_chunks]
-    shared = tp_scatter([after(c, *both_parts[1:]) for c in shared], tp)
+    shared = tp_scatter([after(c, *dtok_parts[1:]) for c in shared], tp)
+    def placed(parts, name, order=()):
+        return call(
+            part(place_rows, tp),
+            [sds((fmax, seqs, width))],
+            far(parts),
+            work=[sds((tp, own, width))],
+            smem=[rank],
+            order=order,
+            name=name,
+        )[0]
+
+    d_tokens = placed(dtok_parts, "place_tokens", [grad_up])
     (block,) = call(
         part(join_rows, keys // nseq, clips),
         [sds((keys // nseq + clip_pad, span))],
         far(shared),
+        order=[d_tokens],
         name="join_rows",
     )
+    out_parts = tp_gather(after(out_own, block), tp)
     blocks = lax.all_gather(block, "seq", axis=0)
-    d_tokens, output = call(
-        part(place_rows, tp),
-        [sds((fmax, seqs, width))] * 2,
-        far(both_parts),
-        work=[sds((tp, 2 * own, width))],
-        smem=[rank],
-        name="place_rows",
-    )
 
     d_caption, d_condition = call(
         part(place_captions, clips),
@@ -1220,10 +1227,11 @@
         [Near(blocks), condition],
         work=[sds((keys, feats)), sds((feats, keys))],
         smem=[cap_len],
-        order=[output, grad_ada],
+        order=[grad_ada],
         name="place_captions",
     )
 
+    output = placed(out_parts, "place_output", [d_caption])
     grad_q2, grad_kv2, grad_out2, grad_qkv, grad_out = call(
         finish_rest,
         [
@@ -1234,7 +1242,7 @@
             sds((drows, inner), F32),
         ],
         [sum_rest],
-        order=[d_caption],
+        order=[output],
         name="finish_rest",
     )
 

time: 321 us -> 312 us (0.972)
  waiting for transfers between devices: 74.7 us -> 65.5 us
    ppermute x18 -> x21, waiting for transfers between devices: 39.3 us -> 31.4 us  [tp_gather(): lax.ppermute(value, 'tp', [(i, (i + k) % tp) for i in range(tp)])]
    ppermute x15, starting transfers between devices: 29.1 us -> 25.2 us  [tp_scatter(): lax.ppermute(chunks[r], 'tp', [(i, (i - r) % tp) for i in range(tp)])]
    ppermute x18 -> x21, starting transfers between devices: 29.7 us -> 33.3 us  [tp_gather(): lax.ppermute(value, 'tp', [(i, (i + k) % tp) for i in range(tp)])]
    pallas_call x22 -> x23, Pallas kernels: 124 us -> 125 us  [call(): pl.pallas_call(kernel, out_shape=tuple((pltpu.HBM(o.shape, o.dtype) for o...]
    unnamed x45 -> x47, local copies, waits for them, and re-layouts: 7.09 us -> 7.1 us
  transfers between devices with their start and end apart: 55 -> 58, of which waited for: 22 -> 22; matrix products, arithmetic and copies ran while one was open for 5% -> 5% of each run, Pallas kernels for 38% -> 39%
where the time goes in v2:
time: 312 us; the launch traced here: 311 us
  Pallas kernels  125 us (40%)
  starting transfers between devices  74.2 us (24%)
  waiting for transfers between devices  65.5 us (21%)
  between operations  14.5 us (5%)
  local copies, waits for them, and re-layouts  12.1 us (4%)
  blocking collectives  11.5 us (4%)
  other arithmetic  7.27 us (2%)
    pallas_call x23, Pallas kernels, call(): pl.pallas_call(kernel, out_shape=tuple((pltpu.HBM(o.shape, o.dtype) for o...  125 us
    ppermute x21, starting transfers between devices, tp_gather(): lax.ppermute(value, 'tp', [(i, (i + k) % tp) for i in range(tp)])  33.3 us
    ppermute x21, waiting for transfers between devices, tp_gather(): lax.ppermute(value, 'tp', [(i, (i + k) % tp) for i in range(tp)])  31.4 us
    ppermute x15, starting transfers between devices, tp_scatter(): lax.ppermute(chunks[r], 'tp', [(i, (i - r) % tp) for i in range(tp)])  25.2 us
    ppermute x15, waiting for transfers between devices, tp_scatter(): lax.ppermute(chunks[r], 'tp', [(i, (i - r) % tp) for i in range(tp)])  19.4 us
    ppermute x17, starting transfers between devices, seq_xor(): return lax.ppermute(value, 'seq', [(i, i ^ mask) for i in range(nseq)])  15.5 us
    ppermute x17, waiting for transfers between devices, seq_xor(): return lax.ppermute(value, 'seq', [(i, i ^ mask) for i in range(nseq)])  14.5 us
    all_gather x1, blocking collectives, shards(): blocks = lax.all_gather(block, 'seq', axis=0)  11.5 us
  transfers between devices with their start and end apart: 58, of which 22 were waited for; matrix products, arithmetic and copies ran while one was open for 5% of the time, Pallas kernels for 39%

profile of v2, /device:TPU:0, one launch (start us, length us, event | category | flops | bytes accessed | tf_op | source)
XLA Modules:
  0.0 311.3 jit_solution(7330755133168732012)
XLA Ops:
  40.9 7.1 %collective-permute-done.8.refs_12_.refs_17_ = bf16[144,1152]{1,0:T(8,128)(2,1)S(1)} collective-permute-done((bf16[144,1152]{1,0:T(8,128)(2,1)S(1)}, bf16[144,1152]{1,0:T(8,128)(2,1)S(1)}, u32[]{:S(2)}, u32[]{:S(2)}) %collective-permute-start.8) | collective-permute-done | bytes 331808 | tf_op jit(solution)/shard_map/ppermute | solution.py:861
  56.2 8.9 %frame_forward.1 = (bf16[288,1152]{1,0:T(8,128)(2,1)}, bf16[288,864]{1,0:T(8,128)(2,1)}, bf16[4,288,288]{2,1,0:T(8,128)(2,1)}, bf16[288,288]{1,0:T(8,128)(2,1)},...) custom-call(s32[2]{0:T(128)S(1)} %pad_add_fusion.refs_0_, ...), custom_call_target="tpu_custom_call" | custom-call | bytes 6204672 | tf_op jit(solution)/shard_map/frame_forward/pallas_call | solution.py:180
  71.4 7.6 %live_captions.1 = (bf16[640,1152]{1,0:T(8,128)(2,1)}, s32[1,640]{1,0:T(1,128)}) custom-call(s32[4]{0:T(128)S(1)} %copy-done, bf16[4,300,1152]{2,1,0:T(8,128)(2,1)} %copy.31.refs_1_), custom_call_target="tpu_custom_call" | custom-call | bytes 4241920 | tf_op jit(solution)/shard_map/live_captions/pallas_call | solution.py:180
  79.0 4.1 %collective-permute-done.14.refs_2_ = bf16[72,1152]{1,0:T(8,128)(2,1)S(1)} collective-permute-done((bf16[72,1152]{1,0:T(8,128)(2,1)}, bf16[72,1152]{1,0:T(8,128)(2,1)S(1)}, u32[]{:S(2)}, u32[]{:S(2)}) %collective-permute-start.14) | collective-permute-done | bytes 165920 | tf_op jit(solution)/shard_map/ppermute | solution.py:856
  91.3 4.9 %key_values.1.refs_7_ = bf16[640,576]{1,0:T(8,128)(2,1)} custom-call(bf16[640,1152]{1,0:T(8,128)(2,1)} %get-tuple-element.120.refs_7_.refs_0_.refs_2_, bf16[1152,960]{1,0:T(8,128)(2,1)} %all-gather.5.cloned.1.call-done.refs_1_.refs_6_.refs_5_), custom_call_target="tpu_custom_call" | custom-call | bytes 4423680 | tf_op jit(solution)/shard_map/key_values/pallas_call | solution.py:180
  96.2 4.4 %collective-permute-done.17.refs_2_ = bf16[72,1152]{1,0:T(8,128)(2,1)S(1)} collective-permute-done((bf16[72,1152]{1,0:T(8,128)(2,1)}, bf16[72,1152]{1,0:T(8,128)(2,1)S(1)}, u32[]{:S(2)}, u32[]{:S(2)}) %collective-permute-start.17) | collective-permute-done | bytes 165920 | tf_op jit(solution)/shard_map/ppermute | solution.py:850
  100.7 7.6 %cross_forward.1 = (bf16[288,1152]{1,0:T(8,128)(2,1)}, bf16[288,288]{1,0:T(8,128)(2,1)}, bf16[4,288,640]{2,1,0:T(8,128)(2,1)}, bf16[288,288]{1,0:T(8,128)(2,1)}, bf16[72,1152]{1,0:T(8,128)(2,1)}) custom-call(bf16[72,1152]{1,0:T(8,128)(2,1)} %get-tuple-element.121.refs_0_, bf16[72,1152]{1,0:T(8,128)(2,1)S(1)} %collective-permute-done.16.refs_1_, ...), custom_call_target="tpu_custom_call" | custom-call | bytes 6252160 | tf_op jit(solution)/shard_map/cross_forward/pallas_call | solution.py:180
  114.4 4.7 %collective-permute-done.19.refs_2_ = bf16[72,1152]{1,0:T(8,128)(2,1)S(1)} collective-permute-done((bf16[72,1152]{1,0:T(8,128)(2,1)}, bf16[72,1152]{1,0:T(8,128)(2,1)S(1)}, u32[]{:S(2)}, u32[]{:S(2)}) %collective-permute-start.19) | collective-permute-done | bytes 165920 | tf_op jit(solution)/shard_map/ppermute | solution.py:850
  119.1 5.1 %collective-permute-done.20.refs_3_ = bf16[72,1152]{1,0:T(8,128)(2,1)S(1)} collective-permute-done((bf16[72,1152]{1,0:T(8,128)(2,1)}, bf16[72,1152]{1,0:T(8,128)(2,1)S(1)}, u32[]{:S(2)}, u32[]{:S(2)}) %collective-permute-start.20) | collective-permute-done | bytes 165920 | tf_op jit(solution)/shard_map/ppermute | solution.py:850
  124.2 12.5 %mlp_both.1 = (f32[72,1152]{1,0:T(8,128)}, bf16[288,1152]{1,0:T(8,128)(2,1)}, bf16[288,1152]{1,0:T(8,128)(2,1)}, bf16[288,1152]{1,0:T(8,128)(2,1)}, bf16[288,115...) custom-call(s32[2]{0:T(128)S(1)} %pad_add_fusion.refs_0_, ...), custom_call_target="tpu_custom_call" | custom-call | bytes 30795264 | tf_op jit(solution)/shard_map/mlp_both/pallas_call | solution.py:180
  136.7 5.2 %collective-permute-start.22 = (bf16[72,1152]{1,0:T(8,128)(2,1)}, bf16[72,1152]{1,0:T(8,128)(2,1)S(1)}, u32[]{:S(2)}, u32[]{:S(2)}) collective-permute-start(bf16[72,1152]{1,0:T(8,128)(2,1)} %get-tuple-element.130), channel_id=1, source_target_pairs={{0,3},{1,0},{2,1},{3,2},{4,7},{5,4},{6,5},{7,6},{8,11},{9,8},{10,9... | collective-permute-start | bytes 497672 | tf_op jit(solution)/shard_map/ppermute | solution.py:856
  142.6 9.0 %grads_mlp.1.refs_9_ = bf16[1152,2304]{1,0:T(8,128)(2,1)} custom-call(bf16[288,1152]{1,0:T(8,128)(2,1)} %get-tuple-element.134.refs_0_, bf16[288,1152]{1,0:T(8,128)(2,1)} %get-tuple-element.135.refs_1_, bf16[288,1152]{1,0:T(8,128)(2,1)} %get-tuple-element.136.refs_2_, bf16[288,1152]{1,0:T(8,128)(2,1)} %get-tuple-element.137.refs_3_), custom_call_target="tpu_custom_call" | custom-call | bytes 7962624 | tf_op jit(solution)/shard_map/grads_mlp/pallas_call | solution.py:180
  151.6 5.7 %collective-permute-done.23.refs_2_ = bf16[72,1152]{1,0:T(8,128)(2,1)S(1)} collective-permute-done((bf16[72,1152]{1,0:T(8,128)(2,1)}, bf16[72,1152]{1,0:T(8,128)(2,1)S(1)}, u32[]{:S(2)}, u32[]{:S(2)}) %collective-permute-start.23) | collective-permute-done | bytes 165920 | tf_op jit(solution)/shard_map/ppermute | solution.py:856
  164.9 5.2 %collective-permute-done.25.refs_2_ = bf16[72,1152]{1,0:T(8,128)(2,1)S(1)} collective-permute-done((bf16[72,1152]{1,0:T(8,128)(2,1)S(1)}, bf16[72,1152]{1,0:T(8,128)(2,1)S(1)}, u32[]{:S(2)}, u32[]{:S(2)}) %collective-permute-start.25) | collective-permute-done | bytes 165920 | tf_op jit(solution)/shard_map/ppermute | solution.py:850
  170.1 5.4 %collective-permute-done.26.refs_3_ = bf16[72,1152]{1,0:T(8,128)(2,1)S(1)} collective-permute-done((bf16[72,1152]{1,0:T(8,128)(2,1)S(1)}, bf16[72,1152]{1,0:T(8,128)(2,1)S(1)}, u32[]{:S(2)}, u32[]{:S(2)}) %collective-permute-start.26) | collective-permute-done | bytes 165920 | tf_op jit(solution)/shard_map/ppermute | solution.py:850
  175.5 10.1 %cross_back.1 = (bf16[288,1152]{1,0:T(8,128)(2,1)}, bf16[288,288]{1,0:T(8,128)(2,1)}, bf16[640,576]{1,0:T(8,128)(2,1)}, bf16[72,1152]{1,0:T(8,128)(2,1)}, bf16[4...) custom-call(s32[2]{0:T(128)S(1)} %pad_add_fusion.refs_0_, bf16[72,1152]{1,0:T(8,128)(2,1)} %get-tuple-element.138.refs_1_, ...), custom_call_target="tpu_custom_call" | custom-call | bytes 13473792 | tf_op jit(solution)/shard_map/cross_back/pallas_call | solution.py:180
  191.3 9.0 %grads_cross.1 = bf16[1152,2304]{1,0:T(8,128)(2,1)} custom-call(bf16[288,1152]{1,0:T(8,128)(2,1)} %get-tuple-element.127.refs_10_.refs_0_, bf16[288,288]{1,0:T(8,128)(2,1)} %get-tuple-element.153.refs_1_, bf16[640,1152]{1,0:T(8,128)(2,1)} %get-tuple-element.120.refs_7_.refs_0_.refs_2_, bf16[640,576]{1,0:T(8,128)(2,1)} %get-tuple-element.154.refs_3_, ...), custom_call_target="tpu_custom_call" | custom-call | bytes 9179136 | tf_op jit(solution)/shard_map/grads_cross/pallas_call | solution.py:180
  201.6 5.3 %collective-permute-start.32 = (bf16[72,1152]{1,0:T(8,128)(2,1)S(1)}, bf16[72,1152]{1,0:T(8,128)(2,1)S(1)}, u32[]{:S(2)}, u32[]{:S(2)}) collective-permute-start(bf16[72,1152]{1,0:T(8,128)(2,1)S(1)} %copy-done.19), channel_id=1, source_target_pairs={{0,3},{1,0},{2,1},{3,2},{4,7},{5,4},{6,5},{7,6},{8,11},{9,8},{10,9... | collective-permute-start | bytes 497672 | tf_op jit(solution)/shard_map/ppermute | solution.py:856
  207.7 13.5 %frame_back.1 = (f32[72,1152]{1,0:T(8,128)}, bf16[288,1152]{1,0:T(8,128)(2,1)}, bf16[288,864]{1,0:T(8,128)(2,1)}, bf16[88,1152]{1,0:T(8,128)(2,1)}, bf16[88,1152...) custom-call(s32[2]{0:T(128)S(1)} %pad_add_fusion.refs_0_, ...), custom_call_target="tpu_custom_call" | custom-call | bytes 13321728 | tf_op jit(solution)/shard_map/frame_back/pallas_call | solution.py:180
  228.2 7.4 %grads_frame.1.refs_14_ = bf16[1152,2304]{1,0:T(8,128)(2,1)} custom-call(bf16[288,1152]{1,0:T(8,128)(2,1)} %get-tuple-element.172.refs_0_, bf16[288,864]{1,0:T(8,128)(2,1)} %get-tuple-element.173.refs_1_, bf16[288,1152]{1,0:T(8,128)(2,1)} %get-tuple-element.174.refs_2_, bf16[288,288]{1,0:T(8,128)(2,1)} %get-tuple-element.175.refs_3_, ...), custom_call_target="tpu_custom_call", output_to_operand_aliasing={{}: (4, {})} | custom-call | bytes 7299072 | tf_op jit(solution)/shard_map/grads_frame/pallas_call | solution.py:180
  235.6 7.2 %collective-permute-done.36.refs_2_ = bf16[88,1152]{1,0:T(8,128)(2,1)S(1)} collective-permute-done((bf16[88,1152]{1,0:T(8,128)(2,1)}, bf16[88,1152]{1,0:T(8,128)(2,1)S(1)}, u32[]{:S(2)}, u32[]{:S(2)}) %collective-permute-start.36) | collective-permute-done | bytes 202784 | tf_op jit(solution)/shard_map/ppermute | solution.py:856
  251.0 4.2 %collective-permute-done.42 = f32[8,1728]{1,0:T(8,128)S(1)} collective-permute-done((f32[8,1728]{1,0:T(8,128)S(1)}, f32[8,1728]{1,0:T(8,128)S(1)}, u32[]{:S(2)}, u32[]{:S(2)}) %collective-permute-start.42) | collective-permute-done | bytes 55328 | tf_op jit(solution)/shard_map/ppermute | solution.py:861
  283.6 11.5 %all-gather = bf16[704,288]{1,0:T(8,128)(2,1)S(1)} all-gather(bf16[88,288]{1,0:T(8,128)(2,1)} %join_rows.1), channel_id=2, replica_groups=mesh['seq'=8,'tp'=4] {'seq'}, dimensions={0}, use_global_device_ids=true | all-gather | bytes 456192 | tf_op jit(solution)/shard_map/all_gather | solution.py:1222
  295.1 4.3 %place_captions.1 = (f32[4,288,300]{2,1,0:T(8,128)}, f32[4,1152]{1,0:T(4,128)}) custom-call(s32[4]{0:T(128)S(1)} %copy-done, bf16[8,88,288]{2,1,0:T(8,128)(2,1)S(1)} %bitcast.26, f32[4,1152]{1,0:T(4,128)} %refs_2_.5, f32[144,1728]{1,0:T(8,128)} %get-tuple-element.106.refs_3_), custom_call_target="tpu_custom_call" | custom-call | bytes 1824768 | tf_op jit(solution)/shard_map/place_captions/pallas_call | solution.py:180
  (197 shorter events, 126.7 us)
Async XLA Ops:
  7.2 84.1 %all-gather.5.cloned.1.call-start = ((), (), s32[]{:S(2)}) async-start(), calls=%async_computation.2 | async-start | bytes 2654208 | tf_op jit(solution)/shard_map/all_gather | solution.py:952
  10.1 114.1 %all-gather.7.cloned.1.call-start = ((), (), s32[]{:S(2)}) async-start(), calls=%async_computation.3 | async-start | bytes 8957952 | tf_op jit(solution)/shard_map/all_gather | solution.py:981
  25.0 15.9 %collective-permute-start.6 = (bf16[144,1152]{1,0:T(8,128)(2,1)S(1)}, bf16[144,1152]{1,0:T(8,128)(2,1)S(1)}, u32[]{:S(2)}, u32[]{:S(2)}) collective-permute-start(bf16[144,1152]{1,0:T(8,128)(2,1)S(1)} %pad_maximum_fusion.refs_6_.refs_11_), channel_id=1, source_target_pairs={{0,8},{4,12},{8,0},{12,4},{16,24},{20,28},{24,16},{28,20},{1,9},{5... | collective-permute-start | bytes 995336 | tf_op jit(solution)/shard_map/ppermute | solution.py:861
  28.4 19.5 %collective-permute-start.8 = (bf16[144,1152]{1,0:T(8,128)(2,1)S(1)}, bf16[144,1152]{1,0:T(8,128)(2,1)S(1)}, u32[]{:S(2)}, u32[]{:S(2)}) collective-permute-start(bf16[144,1152]{1,0:T(8,128)(2,1)S(1)} %pad_maximum_fusion.refs_6_.refs_11_), channel_id=1, source_target_pairs={{0,24},{4,28},{8,16},{12,20},{16,8},{20,12},{24,0},{28,4},{1,25},{... | collective-permute-start | bytes 995336 | tf_op jit(solution)/shard_map/ppermute | solution.py:861
  51.3 156.4 %all-gather.9.cloned.1.call-start = ((), (), s32[]{:S(2)}) async-start(), calls=%async_computation.4 | async-start | bytes 2322432 | tf_op jit(solution)/shard_map/all_gather | solution.py:982
  52.2 219.3 %reduce-scatter.3.cloned.1.call-start = ((), (), s32[]{:S(2)}) async-start(), calls=%async_computation.5 | async-start | bytes 5971968 | tf_op jit(solution)/shard_map/reduce_scatter | solution.py:1081
  68.3 14.8 %collective-permute-start.14 = (bf16[72,1152]{1,0:T(8,128)(2,1)}, bf16[72,1152]{1,0:T(8,128)(2,1)S(1)}, u32[]{:S(2)}, u32[]{:S(2)}) collective-permute-start(bf16[72,1152]{1,0:T(8,128)(2,1)} %get-tuple-element.118), channel_id=1, source_target_pairs={{0,2},{1,3},{2,0},{3,1},{4,6},{5,7},{6,4},{7,5},{8,10},{9,11},{10,... | collective-permute-start | bytes 497672 | tf_op jit(solution)/shard_map/ppermute | solution.py:856
  68.3 14.8 %collective-permute-start.15 = (bf16[72,1152]{1,0:T(8,128)(2,1)}, bf16[72,1152]{1,0:T(8,128)(2,1)S(1)}, u32[]{:S(2)}, u32[]{:S(2)}) collective-permute-start(bf16[72,1152]{1,0:T(8,128)(2,1)} %get-tuple-element.119), channel_id=1, source_target_pairs={{0,1},{1,2},{2,3},{3,0},{4,5},{5,6},{6,7},{7,4},{8,9},{9,10},{10,1... | collective-permute-start | bytes 497672 | tf_op jit(solution)/shard_map/ppermute | solution.py:856
  136.7 14.9 %collective-permute-start.22 = (bf16[72,1152]{1,0:T(8,128)(2,1)}, bf16[72,1152]{1,0:T(8,128)(2,1)S(1)}, u32[]{:S(2)}, u32[]{:S(2)}) collective-permute-start(bf16[72,1152]{1,0:T(8,128)(2,1)} %get-tuple-element.130), channel_id=1, source_target_pairs={{0,3},{1,0},{2,1},{3,2},{4,7},{5,4},{6,5},{7,6},{8,11},{9,8},{10,9... | collective-permute-start | bytes 497672 | tf_op jit(solution)/shard_map/ppermute | solution.py:856
  142.0 15.4 %collective-permute-start.23 = (bf16[72,1152]{1,0:T(8,128)(2,1)}, bf16[72,1152]{1,0:T(8,128)(2,1)S(1)}, u32[]{:S(2)}, u32[]{:S(2)}) collective-permute-start(bf16[72,1152]{1,0:T(8,128)(2,1)} %get-tuple-element.131), channel_id=1, source_target_pairs={{0,2},{1,3},{2,0},{3,1},{4,6},{5,7},{6,4},{7,5},{8,10},{9,11},{10,... | collective-permute-start | bytes 497672 | tf_op jit(solution)/shard_map/ppermute | solution.py:856
  142.3 15.1 %collective-permute-start.24 = (bf16[72,1152]{1,0:T(8,128)(2,1)}, bf16[72,1152]{1,0:T(8,128)(2,1)S(1)}, u32[]{:S(2)}, u32[]{:S(2)}) collective-permute-start(bf16[72,1152]{1,0:T(8,128)(2,1)} %get-tuple-element.132), channel_id=1, source_target_pairs={{0,1},{1,2},{2,3},{3,0},{4,5},{5,6},{6,7},{7,4},{8,9},{9,10},{10,1... | collective-permute-start | bytes 497672 | tf_op jit(solution)/shard_map/ppermute | solution.py:856
  160.2 141.8 %reduce-scatter.5.cloned.1.call-start = ((), (), s32[]{:S(2)}) async-start(), calls=%async_computation.6 | async-start | bytes 5971968 | tf_op jit(solution)/shard_map/reduce_scatter | solution.py:1161
  161.1 14.4 %collective-permute-start.26 = (bf16[72,1152]{1,0:T(8,128)(2,1)S(1)}, bf16[72,1152]{1,0:T(8,128)(2,1)S(1)}, u32[]{:S(2)}, u32[]{:S(2)}) collective-permute-start(bf16[72,1152]{1,0:T(8,128)(2,1)S(1)} %copy-done.15), channel_id=1, source_target_pairs={{0,2},{1,3},{2,0},{3,1},{4,6},{5,7},{6,4},{7,5},{8,10},{9,11},{10,... | collective-permute-start | bytes 497672 | tf_op jit(solution)/shard_map/ppermute | solution.py:850
  185.6 21.9 %collective-permute-start.31 = (bf16[4,80,576]{2,1,0:T(8,128)(2,1)}, bf16[4,80,576]{2,1,0:T(8,128)(2,1)S(1)}, u32[]{:S(2)}, u32[]{:S(2)}) collective-permute-start(bf16[4,80,576]{2,1,0:T(8,128)(2,1)} %get-tuple-element.150), channel_id=1, source_target_pairs={{0,4},{4,0},{8,12},{12,8},{16,20},{20,16},{24,28},{28,24},{1,5},{5... | collective-permute-start | bytes 1105928 | tf_op jit(solution)/shard_map/ppermute | solution.py:861
  185.7 14.6 %collective-permute-start.28 = (bf16[72,1152]{1,0:T(8,128)(2,1)}, bf16[72,1152]{1,0:T(8,128)(2,1)S(1)}, u32[]{:S(2)}, u32[]{:S(2)}) collective-permute-start(bf16[72,1152]{1,0:T(8,128)(2,1)} %get-tuple-element.141.refs_1_), channel_id=1, source_target_pairs={{0,1},{1,2},{2,3},{3,0},{4,5},{5,6},{6,7},{7,4},{8,9},{9,10},{10,1... | collective-permute-start | bytes 497672 | tf_op jit(solution)/shard_map/ppermute | solution.py:850
  201.6 19.7 %collective-permute-start.32 = (bf16[72,1152]{1,0:T(8,128)(2,1)S(1)}, bf16[72,1152]{1,0:T(8,128)(2,1)S(1)}, u32[]{:S(2)}, u32[]{:S(2)}) collective-permute-start(bf16[72,1152]{1,0:T(8,128)(2,1)S(1)} %copy-done.19), channel_id=1, source_target_pairs={{0,3},{1,0},{2,1},{3,2},{4,7},{5,4},{6,5},{7,6},{8,11},{9,8},{10,9... | collective-permute-start | bytes 497672 | tf_op jit(solution)/shard_map/ppermute | solution.py:856
  206.9 15.0 %collective-permute-start.33 = (bf16[72,1152]{1,0:T(8,128)(2,1)S(1)}, bf16[72,1152]{1,0:T(8,128)(2,1)S(1)}, u32[]{:S(2)}, u32[]{:S(2)}) collective-permute-start(bf16[72,1152]{1,0:T(8,128)(2,1)S(1)} %copy-done.18), channel_id=1, source_target_pairs={{0,2},{1,3},{2,0},{3,1},{4,6},{5,7},{6,4},{7,5},{8,10},{9,11},{10,... | collective-permute-start | bytes 497672 | tf_op jit(solution)/shard_map/ppermute | solution.py:856
  207.1 14.8 %collective-permute-start.34 = (bf16[72,1152]{1,0:T(8,128)(2,1)S(1)}, bf16[72,1152]{1,0:T(8,128)(2,1)S(1)}, u32[]{:S(2)}, u32[]{:S(2)}) collective-permute-start(bf16[72,1152]{1,0:T(8,128)(2,1)S(1)} %copy-done.17), channel_id=1, source_target_pairs={{0,1},{1,2},{2,3},{3,0},{4,5},{5,6},{6,7},{7,4},{8,9},{9,10},{10,1... | collective-permute-start | bytes 497672 | tf_op jit(solution)/shard_map/ppermute | solution.py:856
  224.8 18.0 %collective-permute-start.36 = (bf16[88,1152]{1,0:T(8,128)(2,1)}, bf16[88,1152]{1,0:T(8,128)(2,1)S(1)}, u32[]{:S(2)}, u32[]{:S(2)}) collective-permute-start(bf16[88,1152]{1,0:T(8,128)(2,1)} %get-tuple-element.165), channel_id=1, source_target_pairs={{0,2},{1,3},{2,0},{3,1},{4,6},{5,7},{6,4},{7,5},{8,10},{9,11},{10,... | collective-permute-start | bytes 608264 | tf_op jit(solution)/shard_map/ppermute | solution.py:856
  225.7 17.1 %collective-permute-start.37 = (bf16[88,1152]{1,0:T(8,128)(2,1)}, bf16[88,1152]{1,0:T(8,128)(2,1)S(1)}, u32[]{:S(2)}, u32[]{:S(2)}) collective-permute-start(bf16[88,1152]{1,0:T(8,128)(2,1)} %get-tuple-element.167), channel_id=1, source_target_pairs={{0,1},{1,2},{2,3},{3,0},{4,5},{5,6},{6,7},{7,4},{8,9},{9,10},{10,1... | collective-permute-start | bytes 608264 | tf_op jit(solution)/shard_map/ppermute | solution.py:856
  251.0 14.9 %collective-permute-start.44 = (bf16[72,1152]{1,0:T(8,128)(2,1)}, bf16[72,1152]{1,0:T(8,128)(2,1)S(1)}, u32[]{:S(2)}, u32[]{:S(2)}) collective-permute-start(bf16[72,1152]{1,0:T(8,128)(2,1)} %get-tuple-element.177.refs_1_), channel_id=1, source_target_pairs={{0,1},{1,2},{2,3},{3,0},{4,5},{5,6},{6,7},{7,4},{8,9},{9,10},{10,1... | collective-permute-start | bytes 497672 | tf_op jit(solution)/shard_map/ppermute | solution.py:850
  279.7 19.7 %collective-permute-start.50 = (bf16[72,1152]{1,0:T(8,128)(2,1)S(1)}, bf16[72,1152]{1,0:T(8,128)(2,1)S(1)}, u32[]{:S(2)}, u32[]{:S(2)}) collective-permute-start(bf16[72,1152]{1,0:T(8,128)(2,1)S(1)} %copy-done.14), channel_id=1, source_target_pairs={{0,1},{1,2},{2,3},{3,0},{4,5},{5,6},{6,7},{7,4},{8,9},{9,10},{10,1... | collective-permute-start | bytes 497672 | tf_op jit(solution)/shard_map/ppermute | solution.py:850
  280.1 19.3 %collective-permute-start.51 = (bf16[72,1152]{1,0:T(8,128)(2,1)S(1)}, bf16[72,1152]{1,0:T(8,128)(2,1)S(1)}, u32[]{:S(2)}, u32[]{:S(2)}) collective-permute-start(bf16[72,1152]{1,0:T(8,128)(2,1)S(1)} %copy-done.14), channel_id=1, source_target_pairs={{0,2},{1,3},{2,0},{3,1},{4,6},{5,7},{6,4},{7,5},{8,10},{9,11},{10,... | collective-permute-start | bytes 497672 | tf_op jit(solution)/shard_map/ppermute | solution.py:850
  282.4 17.0 %collective-permute-start.52 = (bf16[72,1152]{1,0:T(8,128)(2,1)S(1)}, bf16[72,1152]{1,0:T(8,128)(2,1)S(1)}, u32[]{:S(2)}, u32[]{:S(2)}) collective-permute-start(bf16[72,1152]{1,0:T(8,128)(2,1)S(1)} %copy-done.14), channel_id=1, source_target_pairs={{0,3},{1,0},{2,1},{3,2},{4,7},{5,4},{6,5},{7,6},{8,11},{9,8},{10,9... | collective-permute-start | bytes 497672 | tf_op jit(solution)/shard_map/ppermute | solution.py:850
  (56 other events, 596.0 us)
Sparse Core Ops, SparseCore 0:
  10.5 38.4 all-gather.4
  51.4 52.7 all-gather.6
  106.1 27.7 all-gather.8
  160.3 54.9 reduce-scatter.2
  243.0 56.4 reduce-scatter.4

commit v3 on v2

--- a/solution.py
+++ b/solution.py
@@ -433,7 +433,7 @@
         for r in range(tp):
             branch_o[r].bufs[0][:, cols] = branch[r * own : (r + 1) * own]
 
-    for_columns(weights.shape[0], last)
+    last(slice(0, weights.shape[0]))
     for out in branch_o:
         out.send()
 

time: 312 us -> 312 us (level)
  no operation moved by 1% of the time
where the time goes in v3:
time: 312 us; the launch traced here: 311 us
  Pallas kernels  125 us (40%)
  starting transfers between devices  73.8 us (24%)
  waiting for transfers between devices  65.7 us (21%)
  between operations  14.5 us (5%)
  local copies, waits for them, and re-layouts  12.1 us (4%)
  blocking collectives  11.5 us (4%)
  other arithmetic  7.27 us (2%)
    pallas_call x23, Pallas kernels, call(): pl.pallas_call(kernel, out_shape=tuple((pltpu.HBM(o.shape, o.dtype) for o...  125 us
    ppermute x21, starting transfers between devices, tp_gather(): lax.ppermute(value, 'tp', [(i, (i + k) % tp) for i in range(tp)])  33.4 us
    ppermute x21, waiting for transfers between devices, tp_gather(): lax.ppermute(value, 'tp', [(i, (i + k) % tp) for i in range(tp)])  31.5 us
    ppermute x15, starting transfers between devices, tp_scatter(): lax.ppermute(chunks[r], 'tp', [(i, (i - r) % tp) for i in range(tp)])  24.9 us
    ppermute x15, waiting for transfers between devices, tp_scatter(): lax.ppermute(chunks[r], 'tp', [(i, (i - r) % tp) for i in range(tp)])  19.6 us
    ppermute x17, starting transfers between devices, seq_xor(): return lax.ppermute(value, 'seq', [(i, i ^ mask) for i in range(nseq)])  15.3 us
    ppermute x17, waiting for transfers between devices, seq_xor(): return lax.ppermute(value, 'seq', [(i, i ^ mask) for i in range(nseq)])  14.6 us
    all_gather x1, blocking collectives, shards(): blocks = lax.all_gather(block, 'seq', axis=0)  11.5 us
  transfers between devices with their start and end apart: 58, of which 22 were waited for; matrix products, arithmetic and copies ran while one was open for 5% of the time, Pallas kernels for 39%

profile of v3, /device:TPU:0, one launch (start us, length us, event | category | flops | bytes accessed | tf_op | source)
XLA Modules:
  0.0 310.7 jit_solution(1042409972740055597)
XLA Ops:
  40.9 7.1 %collective-permute-done.8.refs_12_.refs_17_ = bf16[144,1152]{1,0:T(8,128)(2,1)S(1)} collective-permute-done((bf16[144,1152]{1,0:T(8,128)(2,1)S(1)}, bf16[144,1152]{1,0:T(8,128)(2,1)S(1)}, u32[]{:S(2)}, u32[]{:S(2)}) %collective-permute-start.8) | collective-permute-done | bytes 331808 | tf_op jit(solution)/shard_map/ppermute | solution.py:861
  56.2 8.3 %frame_forward.1 = (bf16[288,1152]{1,0:T(8,128)(2,1)}, bf16[288,864]{1,0:T(8,128)(2,1)}, bf16[4,288,288]{2,1,0:T(8,128)(2,1)}, bf16[288,288]{1,0:T(8,128)(2,1)},...) custom-call(s32[2]{0:T(128)S(1)} %pad_add_fusion.refs_0_, ...), custom_call_target="tpu_custom_call" | custom-call | bytes 6204672 | tf_op jit(solution)/shard_map/frame_forward/pallas_call | solution.py:180
  70.8 7.6 %live_captions.1 = (bf16[640,1152]{1,0:T(8,128)(2,1)}, s32[1,640]{1,0:T(1,128)}) custom-call(s32[4]{0:T(128)S(1)} %copy-done, bf16[4,300,1152]{2,1,0:T(8,128)(2,1)} %copy.31.refs_1_), custom_call_target="tpu_custom_call" | custom-call | bytes 4241920 | tf_op jit(solution)/shard_map/live_captions/pallas_call | solution.py:180
  78.4 4.1 %collective-permute-done.14.refs_2_ = bf16[72,1152]{1,0:T(8,128)(2,1)S(1)} collective-permute-done((bf16[72,1152]{1,0:T(8,128)(2,1)}, bf16[72,1152]{1,0:T(8,128)(2,1)S(1)}, u32[]{:S(2)}, u32[]{:S(2)}) %collective-permute-start.14) | collective-permute-done | bytes 165920 | tf_op jit(solution)/shard_map/ppermute | solution.py:856
  90.7 4.9 %key_values.1.refs_7_ = bf16[640,576]{1,0:T(8,128)(2,1)} custom-call(bf16[640,1152]{1,0:T(8,128)(2,1)} %get-tuple-element.120.refs_7_.refs_0_.refs_2_, bf16[1152,960]{1,0:T(8,128)(2,1)} %all-gather.5.cloned.1.call-done.refs_1_.refs_6_.refs_5_), custom_call_target="tpu_custom_call" | custom-call | bytes 4423680 | tf_op jit(solution)/shard_map/key_values/pallas_call | solution.py:180
  95.6 4.4 %collective-permute-done.17.refs_2_ = bf16[72,1152]{1,0:T(8,128)(2,1)S(1)} collective-permute-done((bf16[72,1152]{1,0:T(8,128)(2,1)}, bf16[72,1152]{1,0:T(8,128)(2,1)S(1)}, u32[]{:S(2)}, u32[]{:S(2)}) %collective-permute-start.17) | collective-permute-done | bytes 165920 | tf_op jit(solution)/shard_map/ppermute | solution.py:850
  100.0 7.6 %cross_forward.1 = (bf16[288,1152]{1,0:T(8,128)(2,1)}, bf16[288,288]{1,0:T(8,128)(2,1)}, bf16[4,288,640]{2,1,0:T(8,128)(2,1)}, bf16[288,288]{1,0:T(8,128)(2,1)}, bf16[72,1152]{1,0:T(8,128)(2,1)}) custom-call(bf16[72,1152]{1,0:T(8,128)(2,1)} %get-tuple-element.121.refs_0_, bf16[72,1152]{1,0:T(8,128)(2,1)S(1)} %collective-permute-done.16.refs_1_, ...), custom_call_target="tpu_custom_call" | custom-call | bytes 6252160 | tf_op jit(solution)/shard_map/cross_forward/pallas_call | solution.py:180
  113.7 4.6 %collective-permute-done.19.refs_2_ = bf16[72,1152]{1,0:T(8,128)(2,1)S(1)} collective-permute-done((bf16[72,1152]{1,0:T(8,128)(2,1)}, bf16[72,1152]{1,0:T(8,128)(2,1)S(1)}, u32[]{:S(2)}, u32[]{:S(2)}) %collective-permute-start.19) | collective-permute-done | bytes 165920 | tf_op jit(solution)/shard_map/ppermute | solution.py:850
  118.3 5.3 %collective-permute-done.20.refs_3_ = bf16[72,1152]{1,0:T(8,128)(2,1)S(1)} collective-permute-done((bf16[72,1152]{1,0:T(8,128)(2,1)}, bf16[72,1152]{1,0:T(8,128)(2,1)S(1)}, u32[]{:S(2)}, u32[]{:S(2)}) %collective-permute-start.20) | collective-permute-done | bytes 165920 | tf_op jit(solution)/shard_map/ppermute | solution.py:850
  123.6 12.7 %mlp_both.1 = (f32[72,1152]{1,0:T(8,128)}, bf16[288,1152]{1,0:T(8,128)(2,1)}, bf16[288,1152]{1,0:T(8,128)(2,1)}, bf16[288,1152]{1,0:T(8,128)(2,1)}, bf16[288,115...) custom-call(s32[2]{0:T(128)S(1)} %pad_add_fusion.refs_0_, ...), custom_call_target="tpu_custom_call" | custom-call | bytes 30795264 | tf_op jit(solution)/shard_map/mlp_both/pallas_call | solution.py:180
  136.3 5.0 %collective-permute-start.22 = (bf16[72,1152]{1,0:T(8,128)(2,1)}, bf16[72,1152]{1,0:T(8,128)(2,1)S(1)}, u32[]{:S(2)}, u32[]{:S(2)}) collective-permute-start(bf16[72,1152]{1,0:T(8,128)(2,1)} %get-tuple-element.130), channel_id=1, source_target_pairs={{0,3},{1,0},{2,1},{3,2},{4,7},{5,4},{6,5},{7,6},{8,11},{9,8},{10,9... | collective-permute-start | bytes 497672 | tf_op jit(solution)/shard_map/ppermute | solution.py:856
  141.9 9.0 %grads_mlp.1.refs_9_ = bf16[1152,2304]{1,0:T(8,128)(2,1)} custom-call(bf16[288,1152]{1,0:T(8,128)(2,1)} %get-tuple-element.134.refs_0_, bf16[288,1152]{1,0:T(8,128)(2,1)} %get-tuple-element.135.refs_1_, bf16[288,1152]{1,0:T(8,128)(2,1)} %get-tuple-element.136.refs_2_, bf16[288,1152]{1,0:T(8,128)(2,1)} %get-tuple-element.137.refs_3_), custom_call_target="tpu_custom_call" | custom-call | bytes 7962624 | tf_op jit(solution)/shard_map/grads_mlp/pallas_call | solution.py:180
  150.9 5.9 %collective-permute-done.23.refs_2_ = bf16[72,1152]{1,0:T(8,128)(2,1)S(1)} collective-permute-done((bf16[72,1152]{1,0:T(8,128)(2,1)}, bf16[72,1152]{1,0:T(8,128)(2,1)S(1)}, u32[]{:S(2)}, u32[]{:S(2)}) %collective-permute-start.23) | collective-permute-done | bytes 165920 | tf_op jit(solution)/shard_map/ppermute | solution.py:856
  164.2 5.2 %collective-permute-done.25.refs_2_ = bf16[72,1152]{1,0:T(8,128)(2,1)S(1)} collective-permute-done((bf16[72,1152]{1,0:T(8,128)(2,1)S(1)}, bf16[72,1152]{1,0:T(8,128)(2,1)S(1)}, u32[]{:S(2)}, u32[]{:S(2)}) %collective-permute-start.25) | collective-permute-done | bytes 165920 | tf_op jit(solution)/shard_map/ppermute | solution.py:850
  169.4 5.4 %collective-permute-done.26.refs_3_ = bf16[72,1152]{1,0:T(8,128)(2,1)S(1)} collective-permute-done((bf16[72,1152]{1,0:T(8,128)(2,1)S(1)}, bf16[72,1152]{1,0:T(8,128)(2,1)S(1)}, u32[]{:S(2)}, u32[]{:S(2)}) %collective-permute-start.26) | collective-permute-done | bytes 165920 | tf_op jit(solution)/shard_map/ppermute | solution.py:850
  174.8 10.2 %cross_back.1 = (bf16[288,1152]{1,0:T(8,128)(2,1)}, bf16[288,288]{1,0:T(8,128)(2,1)}, bf16[640,576]{1,0:T(8,128)(2,1)}, bf16[72,1152]{1,0:T(8,128)(2,1)}, bf16[4...) custom-call(s32[2]{0:T(128)S(1)} %pad_add_fusion.refs_0_, bf16[72,1152]{1,0:T(8,128)(2,1)} %get-tuple-element.138.refs_1_, ...), custom_call_target="tpu_custom_call" | custom-call | bytes 13473792 | tf_op jit(solution)/shard_map/cross_back/pallas_call | solution.py:180
  190.6 9.0 %grads_cross.1 = bf16[1152,2304]{1,0:T(8,128)(2,1)} custom-call(bf16[288,1152]{1,0:T(8,128)(2,1)} %get-tuple-element.127.refs_10_.refs_0_, bf16[288,288]{1,0:T(8,128)(2,1)} %get-tuple-element.153.refs_1_, bf16[640,1152]{1,0:T(8,128)(2,1)} %get-tuple-element.120.refs_7_.refs_0_.refs_2_, bf16[640,576]{1,0:T(8,128)(2,1)} %get-tuple-element.154.refs_3_, ...), custom_call_target="tpu_custom_call" | custom-call | bytes 9179136 | tf_op jit(solution)/shard_map/grads_cross/pallas_call | solution.py:180
  200.9 5.3 %collective-permute-start.32 = (bf16[72,1152]{1,0:T(8,128)(2,1)S(1)}, bf16[72,1152]{1,0:T(8,128)(2,1)S(1)}, u32[]{:S(2)}, u32[]{:S(2)}) collective-permute-start(bf16[72,1152]{1,0:T(8,128)(2,1)S(1)} %copy-done.19), channel_id=1, source_target_pairs={{0,3},{1,0},{2,1},{3,2},{4,7},{5,4},{6,5},{7,6},{8,11},{9,8},{10,9... | collective-permute-start | bytes 497672 | tf_op jit(solution)/shard_map/ppermute | solution.py:856
  207.1 13.5 %frame_back.1 = (f32[72,1152]{1,0:T(8,128)}, bf16[288,1152]{1,0:T(8,128)(2,1)}, bf16[288,864]{1,0:T(8,128)(2,1)}, bf16[88,1152]{1,0:T(8,128)(2,1)}, bf16[88,1152...) custom-call(s32[2]{0:T(128)S(1)} %pad_add_fusion.refs_0_, ...), custom_call_target="tpu_custom_call" | custom-call | bytes 13321728 | tf_op jit(solution)/shard_map/frame_back/pallas_call | solution.py:180
  227.5 7.4 %grads_frame.1.refs_14_ = bf16[1152,2304]{1,0:T(8,128)(2,1)} custom-call(bf16[288,1152]{1,0:T(8,128)(2,1)} %get-tuple-element.172.refs_0_, bf16[288,864]{1,0:T(8,128)(2,1)} %get-tuple-element.173.refs_1_, bf16[288,1152]{1,0:T(8,128)(2,1)} %get-tuple-element.174.refs_2_, bf16[288,288]{1,0:T(8,128)(2,1)} %get-tuple-element.175.refs_3_, ...), custom_call_target="tpu_custom_call", output_to_operand_aliasing={{}: (4, {})} | custom-call | bytes 7299072 | tf_op jit(solution)/shard_map/grads_frame/pallas_call | solution.py:180
  234.9 7.2 %collective-permute-done.36.refs_2_ = bf16[88,1152]{1,0:T(8,128)(2,1)S(1)} collective-permute-done((bf16[88,1152]{1,0:T(8,128)(2,1)}, bf16[88,1152]{1,0:T(8,128)(2,1)S(1)}, u32[]{:S(2)}, u32[]{:S(2)}) %collective-permute-start.36) | collective-permute-done | bytes 202784 | tf_op jit(solution)/shard_map/ppermute | solution.py:856
  250.4 4.2 %collective-permute-done.42 = f32[8,1728]{1,0:T(8,128)S(1)} collective-permute-done((f32[8,1728]{1,0:T(8,128)S(1)}, f32[8,1728]{1,0:T(8,128)S(1)}, u32[]{:S(2)}, u32[]{:S(2)}) %collective-permute-start.42) | collective-permute-done | bytes 55328 | tf_op jit(solution)/shard_map/ppermute | solution.py:861
  283.0 11.5 %all-gather = bf16[704,288]{1,0:T(8,128)(2,1)S(1)} all-gather(bf16[88,288]{1,0:T(8,128)(2,1)} %join_rows.1), channel_id=2, replica_groups=mesh['seq'=8,'tp'=4] {'seq'}, dimensions={0}, use_global_device_ids=true | all-gather | bytes 456192 | tf_op jit(solution)/shard_map/all_gather | solution.py:1222
  294.5 4.3 %place_captions.1 = (f32[4,288,300]{2,1,0:T(8,128)}, f32[4,1152]{1,0:T(4,128)}) custom-call(s32[4]{0:T(128)S(1)} %copy-done, bf16[8,88,288]{2,1,0:T(8,128)(2,1)S(1)} %bitcast.26, f32[4,1152]{1,0:T(4,128)} %refs_2_.5, f32[144,1728]{1,0:T(8,128)} %get-tuple-element.106.refs_3_), custom_call_target="tpu_custom_call" | custom-call | bytes 1824768 | tf_op jit(solution)/shard_map/place_captions/pallas_call | solution.py:180
  (197 shorter events, 126.6 us)
Async XLA Ops:
  7.2 83.5 %all-gather.5.cloned.1.call-start = ((), (), s32[]{:S(2)}) async-start(), calls=%async_computation.2 | async-start | bytes 2654208 | tf_op jit(solution)/shard_map/all_gather | solution.py:952
  10.1 113.5 %all-gather.7.cloned.1.call-start = ((), (), s32[]{:S(2)}) async-start(), calls=%async_computation.3 | async-start | bytes 8957952 | tf_op jit(solution)/shard_map/all_gather | solution.py:981
  25.0 15.9 %collective-permute-start.6 = (bf16[144,1152]{1,0:T(8,128)(2,1)S(1)}, bf16[144,1152]{1,0:T(8,128)(2,1)S(1)}, u32[]{:S(2)}, u32[]{:S(2)}) collective-permute-start(bf16[144,1152]{1,0:T(8,128)(2,1)S(1)} %pad_maximum_fusion.refs_6_.refs_11_), channel_id=1, source_target_pairs={{0,8},{4,12},{8,0},{12,4},{16,24},{20,28},{24,16},{28,20},{1,9},{5... | collective-permute-start | bytes 995336 | tf_op jit(solution)/shard_map/ppermute | solution.py:861
  28.4 19.5 %collective-permute-start.8 = (bf16[144,1152]{1,0:T(8,128)(2,1)S(1)}, bf16[144,1152]{1,0:T(8,128)(2,1)S(1)}, u32[]{:S(2)}, u32[]{:S(2)}) collective-permute-start(bf16[144,1152]{1,0:T(8,128)(2,1)S(1)} %pad_maximum_fusion.refs_6_.refs_11_), channel_id=1, source_target_pairs={{0,24},{4,28},{8,16},{12,20},{16,8},{20,12},{24,0},{28,4},{1,25},{... | collective-permute-start | bytes 995336 | tf_op jit(solution)/shard_map/ppermute | solution.py:861
  51.3 155.7 %all-gather.9.cloned.1.call-start = ((), (), s32[]{:S(2)}) async-start(), calls=%async_computation.4 | async-start | bytes 2322432 | tf_op jit(solution)/shard_map/all_gather | solution.py:982
  52.2 218.7 %reduce-scatter.3.cloned.1.call-start = ((), (), s32[]{:S(2)}) async-start(), calls=%async_computation.5 | async-start | bytes 5971968 | tf_op jit(solution)/shard_map/reduce_scatter | solution.py:1081
  67.7 14.8 %collective-permute-start.14 = (bf16[72,1152]{1,0:T(8,128)(2,1)}, bf16[72,1152]{1,0:T(8,128)(2,1)S(1)}, u32[]{:S(2)}, u32[]{:S(2)}) collective-permute-start(bf16[72,1152]{1,0:T(8,128)(2,1)} %get-tuple-element.118), channel_id=1, source_target_pairs={{0,2},{1,3},{2,0},{3,1},{4,6},{5,7},{6,4},{7,5},{8,10},{9,11},{10,... | collective-permute-start | bytes 497672 | tf_op jit(solution)/shard_map/ppermute | solution.py:856
  67.7 14.8 %collective-permute-start.15 = (bf16[72,1152]{1,0:T(8,128)(2,1)}, bf16[72,1152]{1,0:T(8,128)(2,1)S(1)}, u32[]{:S(2)}, u32[]{:S(2)}) collective-permute-start(bf16[72,1152]{1,0:T(8,128)(2,1)} %get-tuple-element.119), channel_id=1, source_target_pairs={{0,1},{1,2},{2,3},{3,0},{4,5},{5,6},{6,7},{7,4},{8,9},{9,10},{10,1... | collective-permute-start | bytes 497672 | tf_op jit(solution)/shard_map/ppermute | solution.py:856
  136.3 14.6 %collective-permute-start.22 = (bf16[72,1152]{1,0:T(8,128)(2,1)}, bf16[72,1152]{1,0:T(8,128)(2,1)S(1)}, u32[]{:S(2)}, u32[]{:S(2)}) collective-permute-start(bf16[72,1152]{1,0:T(8,128)(2,1)} %get-tuple-element.130), channel_id=1, source_target_pairs={{0,3},{1,0},{2,1},{3,2},{4,7},{5,4},{6,5},{7,6},{8,11},{9,8},{10,9... | collective-permute-start | bytes 497672 | tf_op jit(solution)/shard_map/ppermute | solution.py:856
  141.2 15.5 %collective-permute-start.23 = (bf16[72,1152]{1,0:T(8,128)(2,1)}, bf16[72,1152]{1,0:T(8,128)(2,1)S(1)}, u32[]{:S(2)}, u32[]{:S(2)}) collective-permute-start(bf16[72,1152]{1,0:T(8,128)(2,1)} %get-tuple-element.131), channel_id=1, source_target_pairs={{0,2},{1,3},{2,0},{3,1},{4,6},{5,7},{6,4},{7,5},{8,10},{9,11},{10,... | collective-permute-start | bytes 497672 | tf_op jit(solution)/shard_map/ppermute | solution.py:856
  141.7 15.0 %collective-permute-start.24 = (bf16[72,1152]{1,0:T(8,128)(2,1)}, bf16[72,1152]{1,0:T(8,128)(2,1)S(1)}, u32[]{:S(2)}, u32[]{:S(2)}) collective-permute-start(bf16[72,1152]{1,0:T(8,128)(2,1)} %get-tuple-element.132), channel_id=1, source_target_pairs={{0,1},{1,2},{2,3},{3,0},{4,5},{5,6},{6,7},{7,4},{8,9},{9,10},{10,1... | collective-permute-start | bytes 497672 | tf_op jit(solution)/shard_map/ppermute | solution.py:856
  159.5 141.8 %reduce-scatter.5.cloned.1.call-start = ((), (), s32[]{:S(2)}) async-start(), calls=%async_computation.6 | async-start | bytes 5971968 | tf_op jit(solution)/shard_map/reduce_scatter | solution.py:1161
  160.4 14.4 %collective-permute-start.26 = (bf16[72,1152]{1,0:T(8,128)(2,1)S(1)}, bf16[72,1152]{1,0:T(8,128)(2,1)S(1)}, u32[]{:S(2)}, u32[]{:S(2)}) collective-permute-start(bf16[72,1152]{1,0:T(8,128)(2,1)S(1)} %copy-done.15), channel_id=1, source_target_pairs={{0,2},{1,3},{2,0},{3,1},{4,6},{5,7},{6,4},{7,5},{8,10},{9,11},{10,... | collective-permute-start | bytes 497672 | tf_op jit(solution)/shard_map/ppermute | solution.py:850
  185.0 21.9 %collective-permute-start.31 = (bf16[4,80,576]{2,1,0:T(8,128)(2,1)}, bf16[4,80,576]{2,1,0:T(8,128)(2,1)S(1)}, u32[]{:S(2)}, u32[]{:S(2)}) collective-permute-start(bf16[4,80,576]{2,1,0:T(8,128)(2,1)} %get-tuple-element.150), channel_id=1, source_target_pairs={{0,4},{4,0},{8,12},{12,8},{16,20},{20,16},{24,28},{28,24},{1,5},{5... | collective-permute-start | bytes 1105928 | tf_op jit(solution)/shard_map/ppermute | solution.py:861
  185.1 14.6 %collective-permute-start.28 = (bf16[72,1152]{1,0:T(8,128)(2,1)}, bf16[72,1152]{1,0:T(8,128)(2,1)S(1)}, u32[]{:S(2)}, u32[]{:S(2)}) collective-permute-start(bf16[72,1152]{1,0:T(8,128)(2,1)} %get-tuple-element.141.refs_1_), channel_id=1, source_target_pairs={{0,1},{1,2},{2,3},{3,0},{4,5},{5,6},{6,7},{7,4},{8,9},{9,10},{10,1... | collective-permute-start | bytes 497672 | tf_op jit(solution)/shard_map/ppermute | solution.py:850
  200.9 19.6 %collective-permute-start.32 = (bf16[72,1152]{1,0:T(8,128)(2,1)S(1)}, bf16[72,1152]{1,0:T(8,128)(2,1)S(1)}, u32[]{:S(2)}, u32[]{:S(2)}) collective-permute-start(bf16[72,1152]{1,0:T(8,128)(2,1)S(1)} %copy-done.19), channel_id=1, source_target_pairs={{0,3},{1,0},{2,1},{3,2},{4,7},{5,4},{6,5},{7,6},{8,11},{9,8},{10,9... | collective-permute-start | bytes 497672 | tf_op jit(solution)/shard_map/ppermute | solution.py:856
  206.3 15.0 %collective-permute-start.33 = (bf16[72,1152]{1,0:T(8,128)(2,1)S(1)}, bf16[72,1152]{1,0:T(8,128)(2,1)S(1)}, u32[]{:S(2)}, u32[]{:S(2)}) collective-permute-start(bf16[72,1152]{1,0:T(8,128)(2,1)S(1)} %copy-done.18), channel_id=1, source_target_pairs={{0,2},{1,3},{2,0},{3,1},{4,6},{5,7},{6,4},{7,5},{8,10},{9,11},{10,... | collective-permute-start | bytes 497672 | tf_op jit(solution)/shard_map/ppermute | solution.py:856
  206.4 14.8 %collective-permute-start.34 = (bf16[72,1152]{1,0:T(8,128)(2,1)S(1)}, bf16[72,1152]{1,0:T(8,128)(2,1)S(1)}, u32[]{:S(2)}, u32[]{:S(2)}) collective-permute-start(bf16[72,1152]{1,0:T(8,128)(2,1)S(1)} %copy-done.17), channel_id=1, source_target_pairs={{0,1},{1,2},{2,3},{3,0},{4,5},{5,6},{6,7},{7,4},{8,9},{9,10},{10,1... | collective-permute-start | bytes 497672 | tf_op jit(solution)/shard_map/ppermute | solution.py:856
  224.1 18.0 %collective-permute-start.36 = (bf16[88,1152]{1,0:T(8,128)(2,1)}, bf16[88,1152]{1,0:T(8,128)(2,1)S(1)}, u32[]{:S(2)}, u32[]{:S(2)}) collective-permute-start(bf16[88,1152]{1,0:T(8,128)(2,1)} %get-tuple-element.165), channel_id=1, source_target_pairs={{0,2},{1,3},{2,0},{3,1},{4,6},{5,7},{6,4},{7,5},{8,10},{9,11},{10,... | collective-permute-start | bytes 608264 | tf_op jit(solution)/shard_map/ppermute | solution.py:856
  225.0 17.2 %collective-permute-start.37 = (bf16[88,1152]{1,0:T(8,128)(2,1)}, bf16[88,1152]{1,0:T(8,128)(2,1)S(1)}, u32[]{:S(2)}, u32[]{:S(2)}) collective-permute-start(bf16[88,1152]{1,0:T(8,128)(2,1)} %get-tuple-element.167), channel_id=1, source_target_pairs={{0,1},{1,2},{2,3},{3,0},{4,5},{5,6},{6,7},{7,4},{8,9},{9,10},{10,1... | collective-permute-start | bytes 608264 | tf_op jit(solution)/shard_map/ppermute | solution.py:856
  250.4 14.8 %collective-permute-start.44 = (bf16[72,1152]{1,0:T(8,128)(2,1)}, bf16[72,1152]{1,0:T(8,128)(2,1)S(1)}, u32[]{:S(2)}, u32[]{:S(2)}) collective-permute-start(bf16[72,1152]{1,0:T(8,128)(2,1)} %get-tuple-element.177.refs_1_), channel_id=1, source_target_pairs={{0,1},{1,2},{2,3},{3,0},{4,5},{5,6},{6,7},{7,4},{8,9},{9,10},{10,1... | collective-permute-start | bytes 497672 | tf_op jit(solution)/shard_map/ppermute | solution.py:850
  279.1 19.7 %collective-permute-start.50 = (bf16[72,1152]{1,0:T(8,128)(2,1)S(1)}, bf16[72,1152]{1,0:T(8,128)(2,1)S(1)}, u32[]{:S(2)}, u32[]{:S(2)}) collective-permute-start(bf16[72,1152]{1,0:T(8,128)(2,1)S(1)} %copy-done.14), channel_id=1, source_target_pairs={{0,1},{1,2},{2,3},{3,0},{4,5},{5,6},{6,7},{7,4},{8,9},{9,10},{10,1... | collective-permute-start | bytes 497672 | tf_op jit(solution)/shard_map/ppermute | solution.py:850
  279.5 19.3 %collective-permute-start.51 = (bf16[72,1152]{1,0:T(8,128)(2,1)S(1)}, bf16[72,1152]{1,0:T(8,128)(2,1)S(1)}, u32[]{:S(2)}, u32[]{:S(2)}) collective-permute-start(bf16[72,1152]{1,0:T(8,128)(2,1)S(1)} %copy-done.14), channel_id=1, source_target_pairs={{0,2},{1,3},{2,0},{3,1},{4,6},{5,7},{6,4},{7,5},{8,10},{9,11},{10,... | collective-permute-start | bytes 497672 | tf_op jit(solution)/shard_map/ppermute | solution.py:850
  281.8 17.0 %collective-permute-start.52 = (bf16[72,1152]{1,0:T(8,128)(2,1)S(1)}, bf16[72,1152]{1,0:T(8,128)(2,1)S(1)}, u32[]{:S(2)}, u32[]{:S(2)}) collective-permute-start(bf16[72,1152]{1,0:T(8,128)(2,1)S(1)} %copy-done.14), channel_id=1, source_target_pairs={{0,3},{1,0},{2,1},{3,2},{4,7},{5,4},{6,5},{7,6},{8,11},{9,8},{10,9... | collective-permute-start | bytes 497672 | tf_op jit(solution)/shard_map/ppermute | solution.py:850
  (56 other events, 595.3 us)
Sparse Core Ops, SparseCore 0:
  10.5 38.4 all-gather.4
  51.4 52.7 all-gather.6
  106.1 27.7 all-gather.8
  159.7 55.2 reduce-scatter.2
  242.3 56.5 reduce-scatter.4
